TPU v7x, 32 devices: a whole 2x2x4 slice. The times are simulated.
32 devices in a mesh: seq: 8 (over y, x, core), chan: 4 (over z).
Axes of the slice: x: 2, y: 2, z: 4, core: 2. Of those that a mesh axis runs over, the one named last changes fastest.
Arguments:
- layer_input: bfloat16 [4096, 4096], P('chan', 'seq'), may hold values from -6 to 6
- query_proj: bfloat16 [4096, 4096], P('chan', 'seq'), may hold values from -6 to 6
- key_proj: bfloat16 [4096, 4096], P('chan', 'seq'), may hold values from -6 to 6
- value_proj: bfloat16 [4096, 4096], P('chan', 'seq'), may hold values from -6 to 6
- filter_taps: float32 [8, 4096], P('chan', 'seq'), may hold values from -1 to 1
- grad_out: bfloat16 [4096, 4096], P('chan', 'seq'), may hold values from -6 to 6
Outputs:
- mixed_out: bfloat16 [4096, 4096], P('chan', 'seq')
- grad_query: bfloat16 [4096, 4096], P('chan', 'seq')
- grad_key: bfloat16 [4096, 4096], P('chan', 'seq')
- grad_value: bfloat16 [4096, 4096], P('chan', 'seq')
- filter_grad: float32 [8, 4096], P('chan', 'seq')
- weight_grad: float32 [4096, 4096], P('seq', 'chan')
All inputs are finite; a program needn't handle non-finite values.
Results may differ from a plain program's by a relative error of at most 0.0058.
Values may be sent and summed in bfloat16 or wider, within the bound.
No kernel may reach another device: no remote copies, remote signals or barrier semaphores. Data moves between devices by JAX's collectives and lax.ppermute only.
A program may use at most 128 MiB of HBM per device.

v0:
```python
import functools
import math

import jax
import jax.numpy as jnp
from jax import lax
from jax.experimental import pallas as pl
from jax.experimental.pallas import tpu as pltpu
from jax.sharding import PartitionSpec as P


F32 = jnp.float32
BF16 = jnp.bfloat16
EXTRA = 16
SHARES = (2, 4, 4)


def vmem():
    return pl.BlockSpec(memory_space=pltpu.VMEM)


def smem():
    return pl.BlockSpec(memory_space=pltpu.SMEM)


def call(body, outs, scratch, flops, moved, limit_mib, *args):
    many = len(outs) > 1
    return run_kernel(body, outs, scratch, flops, moved, limit_mib, many, *args)


def run_kernel(body, outs, scratch, flops, moved, limit_mib, many, *args):
    specs = [smem()] + [vmem()] * (len(args) - 1)
    got = pl.pallas_call(
        body,
        out_shape=tuple(outs) if many else outs[0],
        in_specs=specs,
        out_specs=tuple([vmem()] * len(outs)) if many else vmem(),
        scratch_shapes=scratch,
        cost_estimate=pl.CostEstimate(
            flops=int(flops), bytes_accessed=int(moved), transcendentals=0
        ),
        compiler_params=pltpu.CompilerParams(vmem_limit_bytes=limit_mib << 20),
    )(*args)
    return got if many else (got,)


def struct(shape, dtype):
    return jax.ShapeDtypeStruct(shape, dtype)


def dot_nn(a, b):
    return lax.dot_general(a, b, (((1,), (0,)), ((), ())), preferred_element_type=F32)


def dot_nt(a, b):
    return lax.dot_general(a, b, (((1,), (1,)), ((), ())), preferred_element_type=F32)


def exchange_slots(pieces, axis):
    count = len(pieces)
    got = [pieces[0]]
    for k in range(1, count):
        pairs = [(i, i ^ k) for i in range(count)]
        got.append(lax.ppermute(pieces[k], axis, pairs))
    return got


def mixed_body(count, piece, group, ids, key, value, taps, *outs):
    me = ids[0]
    for k in range(count):
        dest = me ^ k
        rows = pl.ds(pl.multiple_of(dest * piece, piece), piece)
        outs[k][0:piece, :] = (key[rows, :].astype(F32) * value[rows, :].astype(F32)).astype(BF16)
        row = taps[pl.ds(dest * piece // group, 1), :]
        outs[k][piece : piece + EXTRA, :] = jnp.broadcast_to(row, (EXTRA, row.shape[1])).astype(BF16)


def upstream_body(count, piece, ids, grad, query, *outs):
    me = ids[0]
    for k in range(count):
        dest = me ^ k
        rows = pl.ds(pl.multiple_of(dest * piece, piece), piece)
        outs[k][...] = (grad[rows, :].astype(F32) * query[rows, :].astype(F32)).astype(BF16)


def conv_body(count, piece, ids, *refs):
    me = ids[0]
    slots = refs[:count]
    outs = refs[count : 2 * count]
    toep = refs[2 * count]
    stacked, taps, acc, before = refs[2 * count + 1 :]
    block = stacked.shape[1]
    for k in range(count):
        pos = me ^ k
        stacked[pl.ds(pl.multiple_of(pos * piece, piece), piece), :] = slots[k][0:piece, :]
        taps[pos] = slots[k][piece : piece + 8, :].astype(F32)
    row_id = lax.broadcasted_iota(jnp.int32, (block, block), 0)
    col_id = lax.broadcasted_iota(jnp.int32, (block, block), 1)
    before[...] = jnp.zeros_like(before)

    def build(n, carry):
        base = jnp.broadcast_to(taps[n][0:1, :], (block, block))
        turned = pltpu.roll(base, 0, 1, stride=1, stride_axis=0)
        toep[n] = jnp.where(col_id >= row_id, turned, before[...]).astype(BF16)
        before[...] = turned
        return carry

    lax.fori_loop(0, count, build, 0)
    acc[...] = dot_nn(stacked[...], toep[0])
    for n in range(1, count):
        rows = (count - n) * piece
        acc[n * piece :, :] += dot_nn(stacked[0:rows, :], toep[n])
    for k in range(count):
        pos = me ^ k
        outs[k][...] = acc[pl.ds(pl.multiple_of(pos * piece, piece), piece), :].astype(BF16)


def back_body(count, piece, ids, *refs):
    me = ids[0]
    ups = refs[:count]
    slots = refs[count : 2 * count]
    toep = refs[2 * count]
    outs = refs[2 * count + 1 : 3 * count + 1]
    up_all, in_all, acc, before, sums = refs[3 * count + 1 :]
    block = up_all.shape[1]
    for k in range(count):
        pos = me ^ k
        rows = pl.ds(pl.multiple_of(pos * piece, piece), piece)
        up_all[rows, :] = ups[k][...]
        in_all[rows, :] = slots[k][0:piece, :]
    acc[...] = dot_nt(up_all[...], toep[0])
    for n in range(1, count):
        rows = (count - n) * piece
        acc[0:rows, :] += dot_nt(up_all[n * piece :, :], toep[n])
    row_id = lax.broadcasted_iota(jnp.int32, (block, block), 0)
    col_id = lax.broadcasted_iota(jnp.int32, (block, block), 1)
    keep = col_id + row_id >= block - 1
    flip = (col_id + row_id == block - 1).astype(BF16)
    turned_in = dot_nt(flip, in_all[...]).astype(BF16)
    before[...] = jnp.zeros_like(before)
    for n in reversed(range(count)):
        rows = (count - n) * piece
        prod = dot_nn(turned_in[:, 0:rows], up_all[n * piece :, :])
        both = jnp.where(keep, prod, before[...])
        before[...] = prod
        lined = pltpu.roll(both, 1, 1, stride=1, stride_axis=0)
        total = jnp.sum(lined, axis=0, keepdims=True)
        sums[n] = jnp.broadcast_to(total, (8, block))
    for k in range(count):
        pos = me ^ k
        outs[k][0:piece, :] = acc[pl.ds(pl.multiple_of(pos * piece, piece), piece), :].astype(BF16)
        full = sums[pos]
        high = full.astype(BF16)
        low = (full - high.astype(F32)).astype(BF16)
        outs[k][piece : piece + EXTRA, :] = jnp.concatenate([high, low], axis=0)


def query_body(count, piece, ids, *refs):
    me = ids[0]
    slots = refs[:count]
    query, grad, mixed, grad_query = refs[count:]
    for k in range(count):
        pos = me ^ k
        rows = pl.ds(pl.multiple_of(pos * piece, piece), piece)
        conv = slots[k][...].astype(F32)
        mixed[rows, :] = (query[rows, :].astype(F32) * conv).astype(BF16)
        grad_query[rows, :] = (grad[rows, :].astype(F32) * conv).astype(BF16)


def key_body(count, piece, group, factor, ids, *refs):
    me = ids[0]
    slots = refs[:count]
    key, value, grad_key, grad_value, taps_grad = refs[count:]
    row_id = lax.broadcasted_iota(jnp.int32, taps_grad.shape, 0)
    total = jnp.zeros(taps_grad.shape, F32)
    for k in range(count):
        pos = me ^ k
        rows = pl.ds(pl.multiple_of(pos * piece, piece), piece)
        back = slots[k][0:piece, :].astype(F32)
        grad_key[rows, :] = (back * value[rows, :].astype(F32)).astype(BF16)
        grad_value[rows, :] = (back * key[rows, :].astype(F32)).astype(BF16)
        tail = slots[k][piece : piece + EXTRA, :].astype(F32)
        row = tail[0:1, :] + tail[8:9, :]
        total = total + jnp.where(row_id == pos * piece // group, row, 0.0)
    taps_grad[...] = total * factor


def weight_body(chans, ids, own_grad, other_grad, *refs):
    chip, plane = ids[0], ids[1]
    own, a1, a2, a3, b1, b2 = refs[:6]
    mine, send_p, send_q, keep_p, keep_q, stack = refs[6:]
    rows = own.shape[1]
    half = mine.shape[1] // 2
    inner = (plane == 1) | (plane == 2)
    outer = jnp.logical_not(inner)
    for r in range(chans):
        apart = (chip ^ r) ^ plane
        choices = (
            (own, apart == 0),
            (a1, apart == 1),
            (b2, (apart == 2) & inner),
            (a2, (apart == 2) & outer),
            (b1, (apart == 3) & inner),
            (a3, (apart == 3) & outer),
        )
        for source, chosen in choices:

            @pl.when(chosen)
            def _(source=source, r=r):
                stack[0, r * rows : (r + 1) * rows, :] = source[0]
                stack[1, r * rows : (r + 1) * rows, :] = source[1]

    def part(r, first):
        a = stack[0, r * rows : (r + 1) * rows, :]
        b = stack[1, r * rows : (r + 1) * rows, :]
        cols = slice(first, first + half)
        return dot_nt(a, own_grad[cols, :]) + dot_nt(b, other_grad[cols, :])

    for side in range(2):
        first = side * half
        send = (send_p, send_q)[side]
        order = (1, 3) if side == 0 else (2, 3)
        for n in range(2):
            send[n] = part(order[n], first).astype(BF16)
        (keep_p, keep_q)[side][...] = part(3 - order[0], first)
        mine[:, first : first + half] = part(0, first)


def middle_body(ids, keep_p, got_p, keep_q, got_q, out_p, out_q):
    out_p[...] = (keep_p[...] + got_p[1].astype(F32)).astype(BF16)
    out_q[...] = (keep_q[...] + got_q[1].astype(F32)).astype(BF16)


def finish_body(chunks, factor, ids, *refs):
    out = refs[-1]
    half = refs[0].shape[1] // 2
    first = 0
    for n in range(chunks):
        mine, got_p, got_q, last_p, last_q = refs[5 * n : 5 * n + 5]
        here = slice(first, first + mine.shape[0])
        first += mine.shape[0]
        left = mine[:, :half] + got_p[0].astype(F32) + last_p[...].astype(F32)
        right = mine[:, half:] + got_q[0].astype(F32) + last_q[...].astype(F32)
        out[here, :half] = left * factor
        out[here, half:] = right * factor


def plane_pairs(seqs, chans):
    outer = [(i, i ^ 1) for i in range(chans)]
    middle = []
    for i in range(seqs):
        for j in range(chans):
            to = (i, j ^ 3) if j in (1, 2) else (i ^ 1, j)
            middle.append((i * chans + j, to[0] * chans + to[1]))
    return outer, middle


def gather_planes(block, seqs, chans):
    outer, middle = plane_pairs(seqs, chans)
    both = ("seq", "chan")
    a1 = lax.ppermute(block, "chan", outer)
    b1 = lax.ppermute(block, both, middle)
    a2 = lax.ppermute(b1, "chan", outer)
    b2 = lax.ppermute(a1, both, middle)
    a3 = lax.ppermute(b2, "chan", outer)
    return [block, a1, a2, a3, b1, b2]


def weight_start(layer_input, seq_id):
    channels, _ = layer_input.shape
    seqs, chans = lax.axis_size("seq"), lax.axis_size("chan")
    half = channels // 2
    core = seq_id & 1
    swap = [(i, i ^ 1) for i in range(seqs)]
    give = lax.dynamic_slice_in_dim(layer_input, (1 - core) * half, half, 0)
    keep = lax.dynamic_slice_in_dim(layer_input, core * half, half, 0)
    other = lax.ppermute(give, "seq", swap)
    gathered = []
    first = 0
    for share in SHARES:
        here = slice(first, first + half // share)
        first += half // share
        gathered.append(gather_planes(jnp.stack([keep[here], other[here]]), seqs, chans))
    return gathered


def weight_finish(gathered, grad_query, seq_id, chan_id, factor):
    seqs, chans = lax.axis_size("seq"), lax.axis_size("chan")
    outputs, tok = grad_query.shape
    half = outputs // 2
    swap = [(i, i ^ 1) for i in range(seqs)]
    along = [(i, i ^ 2) for i in range(seqs)]
    across = [(i, i ^ 4) for i in range(seqs)]
    other_grad = lax.ppermute(grad_query, "seq", swap)
    ids = jnp.stack([seq_id >> 1, chan_id])
    parts = []
    for sources in gathered:
        rows = sources[0].shape[1]
        mine, send_p, send_q, keep_p, keep_q = call(
            functools.partial(weight_body, chans),
            [
                struct((rows, outputs), F32),
                struct((2, rows, half), BF16),
                struct((2, rows, half), BF16),
                struct((rows, half), F32),
                struct((rows, half), F32),
            ],
            [pltpu.VMEM((2, chans * rows, tok), BF16)],
            4 * chans * rows * outputs * tok,
            12 << 20,
            20,
            ids,
            grad_query,
            other_grad,
            *sources,
        )
        got_p = lax.ppermute(send_p, "seq", along)
        got_q = lax.ppermute(send_q, "seq", across)
        next_p, next_q = call(
            middle_body,
            [struct((rows, half), BF16)] * 2,
            [],
            rows * outputs,
            4 << 20,
            8,
            ids,
            keep_p,
            got_p,
            keep_q,
            got_q,
        )
        last_p = lax.ppermute(next_p, "seq", across)
        last_q = lax.ppermute(next_q, "seq", along)
        parts += [mine, got_p, got_q, last_p, last_q]
    (out,) = call(
        functools.partial(finish_body, len(gathered), factor),
        [struct((channels_of(gathered), outputs), F32)],
        [],
        3 * outputs * outputs,
        8 << 20,
        16,
        ids,
        *parts,
    )
    return out


def channels_of(gathered):
    return sum(sources[0].shape[1] for sources in gathered)


def weight_general(layer_input, grad_query, factor):
    gathered = lax.all_gather(layer_input, "chan", axis=0, tiled=True)
    summed = lax.psum_scatter(
        jnp.einsum("it,jt->ij", gathered, grad_query, preferred_element_type=F32),
        "seq",
        scatter_dimension=0,
        tiled=True,
    )
    return summed * factor


def per_device(layer_input, query_proj, key_proj, value_proj, filter_taps, grad_out):
    seqs = lax.axis_size("seq")
    chans = lax.axis_size("chan")
    channels, tok = query_proj.shape
    length = seqs * tok
    piece = channels // seqs
    group = channels // filter_taps.shape[0]
    weight_factor = 1.0 / math.sqrt(length)
    taps_factor = 1.0 / math.sqrt(group * length)
    seq_id = lax.axis_index("seq")
    chan_id = lax.axis_index("chan")
    ids = jnp.stack([seq_id, chan_id])
    special = seqs == 8 and chans == 4
    small = struct((piece, tok), BF16)
    large = struct((piece + EXTRA, tok), BF16)
    flat = pltpu.VMEM((channels, tok), BF16)
    wide = pltpu.VMEM((channels, tok), F32)
    square = pltpu.VMEM((tok, tok), F32)
    rows8 = pltpu.VMEM((seqs, 8, tok), F32)
    unit = channels * tok
    work = unit * tok * (seqs + 1)

    mixed = call(
        functools.partial(mixed_body, seqs, piece, group),
        [large] * seqs, [], 3 * unit, 6 * unit, 16,
        ids, key_proj, value_proj, filter_taps,
    )
    mixed_slots = exchange_slots(mixed, "seq")
    upstream = call(
        functools.partial(upstream_body, seqs, piece),
        [small] * seqs, [], 3 * unit, 6 * unit, 16,
        ids, grad_out, query_proj,
    )
    up_slots = exchange_slots(upstream, "seq")
    if special:
        gathered = weight_start(layer_input, seq_id)
    conv = call(
        functools.partial(conv_body, seqs, piece),
        [small] * seqs + [struct((seqs, tok, tok), BF16)],
        [flat, rows8, wide, square],
        work, 16 * unit, 22,
        ids, *mixed_slots,
    )
    conv_slots = exchange_slots(conv[:seqs], "seq")
    mixed_out, grad_query = call(
        functools.partial(query_body, seqs, piece),
        [struct((channels, tok), BF16)] * 2, [], 4 * unit, 10 * unit, 16,
        ids, *conv_slots, query_proj, grad_out,
    )
    back = call(
        functools.partial(back_body, seqs, piece),
        [large] * seqs,
        [flat, flat, wide, square, rows8],
        2 * work, 20 * unit, 24,
        ids, *up_slots, *mixed_slots, conv[seqs],
    )
    back_slots = exchange_slots(back, "seq")
    grad_key, grad_value, filter_grad = call(
        functools.partial(key_body, seqs, piece, group, taps_factor),
        [struct((channels, tok), BF16)] * 2 + [struct(filter_taps.shape, F32)],
        [], 4 * unit, 10 * unit, 16,
        ids, *back_slots, key_proj, value_proj,
    )
    if special:
        weight_grad = weight_finish(gathered, grad_query, seq_id, chan_id, weight_factor)
    else:
        weight_grad = weight_general(layer_input, grad_query, weight_factor)
    return (mixed_out, grad_query, grad_key, grad_value, filter_grad, weight_grad)


def solution(mesh):
    placed = (P("chan", "seq"),) * 6
    return jax.shard_map(
        per_device,
        mesh=mesh,
        in_specs=placed,
        out_specs=(P("chan", "seq"),) * 5 + (P("seq", "chan"),),
        check_vma=False,
    )
```

profile of v0, /device:TPU:0, one launch (start us, length us, event | category | flops | bytes accessed | tf_op | source)
XLA Modules:
  0.0 188.3 jit_solution(17284078442592629390)
XLA Ops:
  7.1 3.0 %collective-permute-start.1 = (bf16[144,512]{1,0:T(8,128)(2,1)S(1)}, bf16[144,512]{1,0:T(8,128)(2,1)S(1)}, u32[]{:S(2)}, u32[]{:S(2)}) collective-permute-start(bf16[144,512]{1,0:T(8,128)(2,1)S(1)} %get-tuple-element.67), channel_id=1, source_target_pairs={{0,8},{4,12},{8,0},{12,4},{16,24},{20,28},{24,16},{28,20},{1,9},{5... | collective-permute-start | bytes 442376 | tf_op jit(solution)/shard_map/ppermute | solution.py:64
  11.8 2.9 %collective-permute-done.1.refs_2_.refs_10_ = bf16[144,512]{1,0:T(8,128)(2,1)S(1)} collective-permute-done((bf16[144,512]{1,0:T(8,128)(2,1)S(1)}, bf16[144,512]{1,0:T(8,128)(2,1)S(1)}, u32[]{:S(2)}, u32[]{:S(2)}) %collective-permute-start.1) | collective-permute-done | bytes 147488 | tf_op jit(solution)/shard_map/ppermute | solution.py:64
  14.8 3.0 %collective-permute-start.5 = (bf16[144,512]{1,0:T(8,128)(2,1)S(1)}, bf16[144,512]{1,0:T(8,128)(2,1)S(1)}, u32[]{:S(2)}, u32[]{:S(2)}) collective-permute-start(bf16[144,512]{1,0:T(8,128)(2,1)S(1)} %get-tuple-element.71), channel_id=1, source_target_pairs={{0,24},{4,28},{8,16},{12,20},{16,8},{20,12},{24,0},{28,4},{1,25},{... | collective-permute-start | bytes 442376 | tf_op jit(solution)/shard_map/ppermute | solution.py:64
  17.7 2.9 %collective-permute-start.6 = (bf16[144,512]{1,0:T(8,128)(2,1)S(1)}, bf16[144,512]{1,0:T(8,128)(2,1)S(1)}, u32[]{:S(2)}, u32[]{:S(2)}) collective-permute-start(bf16[144,512]{1,0:T(8,128)(2,1)S(1)} %get-tuple-element.72), channel_id=1, source_target_pairs={{0,28},{4,24},{8,20},{12,16},{16,12},{20,8},{24,4},{28,0},{1,29},{... | collective-permute-start | bytes 442376 | tf_op jit(solution)/shard_map/ppermute | solution.py:64
  28.8 4.5 %shard_map.110 = (bf16[128,512]{1,0:T(8,128)(2,1)S(1)}, bf16[128,512]{1,0:T(8,128)(2,1)S(1)}, bf16[128,512]{1,0:T(8,128)(2,1)S(1)}, bf16[128,512]{1,0:T(8,128)(2...) custom-call(s32[2]{0:T(128)S(1)} %pad_add_fusion.ids, ...), custom_call_target="tpu_custom_call" | custom-call | flops 2415919104 | bytes 8388608 | tf_op jit(solution)/shard_map/pallas_call | solution.py:33
  33.5 2.7 %collective-permute-start.19 = (bf16[128,512]{1,0:T(8,128)(2,1)S(1)}, bf16[128,512]{1,0:T(8,128)(2,1)S(1)}, u32[]{:S(2)}, u32[]{:S(2)}) collective-permute-start(bf16[128,512]{1,0:T(8,128)(2,1)S(1)} %get-tuple-element.89), channel_id=1, source_target_pairs={{0,24},{4,28},{8,16},{12,20},{16,8},{20,12},{24,0},{28,4},{1,25},{... | collective-permute-start | bytes 393224 | tf_op jit(solution)/shard_map/ppermute | solution.py:64
  38.4 5.9 %collective-permute-done.18.refs_5_ = bf16[128,512]{1,0:T(8,128)(2,1)S(1)} collective-permute-done((bf16[128,512]{1,0:T(8,128)(2,1)S(1)}, bf16[128,512]{1,0:T(8,128)(2,1)S(1)}, u32[]{:S(2)}, u32[]{:S(2)}) %collective-permute-start.18) | collective-permute-done | bytes 131104 | tf_op jit(solution)/shard_map/ppermute | solution.py:64
  53.1 6.9 %shard_map.113 = (bf16[144,512]{1,0:T(8,128)(2,1)S(1)}, bf16[144,512]{1,0:T(8,128)(2,1)S(1)}, bf16[144,512]{1,0:T(8,128)(2,1)S(1)}, bf16[144,512]{1,0:T(8,128)(2...) custom-call(s32[2]{0:T(128)S(1)} %pad_add_fusion.ids, ...), custom_call_target="tpu_custom_call" | custom-call | flops 4831838208 | bytes 10485760 | tf_op jit(solution)/shard_map/pallas_call | solution.py:33
  61.6 2.3 %shard_map.111 = (bf16[1024,512]{1,0:T(8,128)(2,1)}, bf16[1024,512]{1,0:T(8,128)(2,1)}) custom-call(s32[2]{0:T(128)S(1)} %pad_add_fusion.ids, bf16[128,512]{1,0:T(8,128)(2,1)S(1)} %get-tuple-element.73.refs_0_, bf16[128,512]{1,0:T(8,128)(2,1)S(1)} %collective-permute-done.7.refs_1_, bf16[128,512]{1,0:T(8,128)(2,1)S(1)} %collective-permute-done.8.refs_2_, ...), custom_call_target="tpu_custom_call" | custom-call | flops 2097152 | bytes 5242880 | tf_op jit(solution)/shard_map/pallas_call | solution.py:33
  65.3 2.7 %collective-permute-start.39 = (bf16[2,128,512]{2,1,0:T(8,128)(2,1)S(1)}, bf16[2,128,512]{2,1,0:T(8,128)(2,1)}, u32[]{:S(2)}, u32[]{:S(2)}) collective-permute-start(bf16[2,128,512]{2,1,0:T(8,128)(2,1)S(1)} %pad_maximum_fusion.1.refs_0_), channel_id=1, source_target_pairs={{0,1},{1,0},{2,3},{3,2},{4,5},{5,4},{6,7},{7,6},{8,9},{9,8},{10,11... | collective-permute-start | bytes 786440 | tf_op jit(solution)/shard_map/ppermute | solution.py:261
  68.0 6.3 %collective-permute-done.39.refs_1_ = bf16[2,128,512]{2,1,0:T(8,128)(2,1)} collective-permute-done((bf16[2,128,512]{2,1,0:T(8,128)(2,1)S(1)}, bf16[2,128,512]{2,1,0:T(8,128)(2,1)}, u32[]{:S(2)}, u32[]{:S(2)}) %collective-permute-start.39) | collective-permute-done | bytes 262176 | tf_op jit(solution)/shard_map/ppermute | solution.py:261
  76.1 22.4 %collective-permute-start.32 = (bf16[2,256,512]{2,1,0:T(8,128)(2,1)}, bf16[2,256,512]{2,1,0:T(8,128)(2,1)}, u32[]{:S(2)}, u32[]{:S(2)}) collective-permute-start(bf16[2,256,512]{2,1,0:T(8,128)(2,1)} %collective-permute-done.31.refs_4_), channel_id=1, source_target_pairs={{0,1},{1,0},{2,3},{3,2},{4,5},{5,4},{6,7},{7,6},{8,9},{9,8},{10,11... | collective-permute-start | bytes 1572872 | tf_op jit(solution)/shard_map/ppermute | solution.py:263
  100.5 11.2 %collective-permute-start.41 = (bf16[2,128,512]{2,1,0:T(8,128)(2,1)}, bf16[2,128,512]{2,1,0:T(8,128)(2,1)S(1)}, u32[]{:S(2)}, u32[]{:S(2)}) collective-permute-start(bf16[2,128,512]{2,1,0:T(8,128)(2,1)} %copy-done.13), channel_id=1, source_target_pairs={{0,1},{1,0},{2,3},{3,2},{4,5},{5,4},{6,7},{7,6},{8,9},{9,8},{10,11... | collective-permute-start | bytes 786440 | tf_op jit(solution)/shard_map/ppermute | solution.py:263
  111.7 4.1 %collective-permute-start.43 = (bf16[2,128,512]{2,1,0:T(8,128)(2,1)}, bf16[2,128,512]{2,1,0:T(8,128)(2,1)S(1)}, u32[]{:S(2)}, u32[]{:S(2)}) collective-permute-start(bf16[2,128,512]{2,1,0:T(8,128)(2,1)} %collective-permute-done.42.refs_5_), channel_id=1, source_target_pairs={{0,1},{1,0},{2,3},{3,2},{4,5},{5,4},{6,7},{7,6},{8,9},{9,8},{10,11... | collective-permute-start | bytes 786440 | tf_op jit(solution)/shard_map/ppermute | solution.py:265
  116.0 6.9 %collective-permute-done.34.refs_3_ = bf16[2,256,512]{2,1,0:T(8,128)(2,1)} collective-permute-done((bf16[2,256,512]{2,1,0:T(8,128)(2,1)}, bf16[2,256,512]{2,1,0:T(8,128)(2,1)}, u32[]{:S(2)}, u32[]{:S(2)}) %collective-permute-start.34) | collective-permute-done | bytes 524320 | tf_op jit(solution)/shard_map/ppermute | solution.py:265
  126.1 4.4 %shard_map.115 = (f32[256,1024]{1,0:T(8,128)S(1)}, bf16[2,256,512]{2,1,0:T(8,128)(2,1)S(1)}, bf16[2,256,512]{2,1,0:T(8,128)(2,1)S(1)}, f32[256,512]{1,0:T(8,128)S(1)}, f32[256,512]{1,0:T(8,128)S(1)}) custom-call(s32[2]{0:T(128)S(1)} %pad_add_fusion.1.ids, bf16[1024,512]{1,0:T(8,128)(2,1)S(1)} %copy-done.9, ...), custom_call_target="tpu_custom_call" | custom-call | flops 2147483648 | bytes 12582912 | tf_op jit(solution)/shard_map/pallas_call | solution.py:33
  134.9 4.0 %shard_map.117 = (f32[128,1024]{1,0:T(8,128)S(1)}, bf16[2,128,512]{2,1,0:T(8,128)(2,1)S(1)}, bf16[2,128,512]{2,1,0:T(8,128)(2,1)S(1)}, f32[128,512]{1,0:T(8,128)S(1)}, f32[128,512]{1,0:T(8,128)S(1)}) custom-call(s32[2]{0:T(128)S(1)} %pad_add_fusion.1.ids, bf16[1024,512]{1,0:T(8,128)(2,1)S(1)} %copy-done.9, ...), custom_call_target="tpu_custom_call" | custom-call | flops 1073741824 | bytes 12582912 | tf_op jit(solution)/shard_map/pallas_call | solution.py:33
  144.8 3.9 %shard_map.119 = (f32[128,1024]{1,0:T(8,128)S(1)}, bf16[2,128,512]{2,1,0:T(8,128)(2,1)S(1)}, bf16[2,128,512]{2,1,0:T(8,128)(2,1)S(1)}, f32[128,512]{1,0:T(8,128)S(1)}, f32[128,512]{1,0:T(8,128)S(1)}) custom-call(s32[2]{0:T(128)S(1)} %pad_add_fusion.1.ids, bf16[1024,512]{1,0:T(8,128)(2,1)S(1)} %copy-done.10, ...), custom_call_target="tpu_custom_call" | custom-call | flops 1073741824 | bytes 12582912 | tf_op jit(solution)/shard_map/pallas_call | solution.py:33
  148.7 4.5 %collective-permute-done.24.refs_4_ = bf16[144,512]{1,0:T(8,128)(2,1)S(1)} collective-permute-done((bf16[144,512]{1,0:T(8,128)(2,1)S(1)}, bf16[144,512]{1,0:T(8,128)(2,1)S(1)}, u32[]{:S(2)}, u32[]{:S(2)}) %collective-permute-start.24) | collective-permute-done | bytes 147488 | tf_op jit(solution)/shard_map/ppermute | solution.py:64
  156.9 2.5 %collective-permute-start.27 = (bf16[144,512]{1,0:T(8,128)(2,1)S(1)}, bf16[144,512]{1,0:T(8,128)(2,1)S(1)}, u32[]{:S(2)}, u32[]{:S(2)}) collective-permute-start(bf16[144,512]{1,0:T(8,128)(2,1)S(1)} %get-tuple-element.99), channel_id=1, source_target_pairs={{0,28},{4,24},{8,20},{12,16},{16,12},{20,8},{24,4},{28,0},{1,29},{... | collective-permute-start | bytes 442376 | tf_op jit(solution)/shard_map/ppermute | solution.py:64
  160.7 9.2 %collective-permute-done.25.refs_5_ = bf16[144,512]{1,0:T(8,128)(2,1)S(1)} collective-permute-done((bf16[144,512]{1,0:T(8,128)(2,1)S(1)}, bf16[144,512]{1,0:T(8,128)(2,1)S(1)}, u32[]{:S(2)}, u32[]{:S(2)}) %collective-permute-start.25) | collective-permute-done | bytes 147488 | tf_op jit(solution)/shard_map/ppermute | solution.py:64
  176.5 2.3 %shard_map.114 = (bf16[1024,512]{1,0:T(8,128)(2,1)}, bf16[1024,512]{1,0:T(8,128)(2,1)}, f32[2,512]{1,0:T(2,128)}) custom-call(s32[2]{0:T(128)S(1)} %pad_add_fusion.ids, bf16[144,512]{1,0:T(8,128)(2,1)S(1)} %get-tuple-element.92.refs_0_, bf16[144,512]{1,0:T(8,128)(2,1)S(1)} %collective-permute-done.21.refs_1_, ...), custom_call_target="tpu_custom_call" | custom-call | flops 2097152 | bytes 5242880 | tf_op jit(solution)/shard_map/pallas_call | solution.py:33
  178.8 5.1 %collective-permute-done.47.refs_9_ = bf16[128,512]{1,0:T(8,128)(2,1)S(1)} collective-permute-done((bf16[128,512]{1,0:T(8,128)(2,1)S(1)}, bf16[128,512]{1,0:T(8,128)(2,1)S(1)}, u32[]{:S(2)}, u32[]{:S(2)}) %collective-permute-start.47) | collective-permute-done | bytes 131104 | tf_op jit(solution)/shard_map/ppermute | solution.py:333
  186.0 2.2 %shard_map.121 = f32[512,1024]{1,0:T(8,128)} custom-call(s32[2]{0:T(128)S(1)} %pad_add_fusion.1.ids, f32[256,1024]{1,0:T(8,128)S(1)} %get-tuple-element.103.refs_0_, bf16[2,256,512]{2,1,0:T(8,128)(2,1)S(1)} %collective-permute-done.35.got_p.refs_1_, bf16[2,256,512]{2,1,0:T(8,128)(2,1)S(1)} %collective-permute-done.36.got_q.refs_2_, ...), custom_call_target="tpu_custom_call" | custom-call | flops 3145728 | bytes 8388608 | tf_op jit(solution)/shard_map/pallas_call | solution.py:33
  (157 shorter events, 61.2 us)
Async XLA Ops:
  2.5 31.0 %collective-permute-start.29 = (bf16[512,512]{1,0:T(8,128)(2,1)}, bf16[512,512]{1,0:T(8,128)(2,1)S(1)}, u32[]{:S(2)}, u32[]{:S(2)}) collective-permute-start(bf16[512,512]{1,0:T(8,128)(2,1)} %constant_dynamic-slice_fusion), channel_id=1, source_target_pairs={{0,4},{4,0},{8,12},{12,8},{16,20},{20,16},{24,28},{28,24},{1,5},{5... | collective-permute-start | bytes 1572872 | tf_op jit(solution)/shard_map/ppermute | solution.py:277
  10.1 14.8 %collective-permute-start.3 = (bf16[144,512]{1,0:T(8,128)(2,1)S(1)}, bf16[144,512]{1,0:T(8,128)(2,1)S(1)}, u32[]{:S(2)}, u32[]{:S(2)}) collective-permute-start(bf16[144,512]{1,0:T(8,128)(2,1)S(1)} %get-tuple-element.69), channel_id=1, source_target_pairs={{0,16},{4,20},{8,24},{12,28},{16,0},{20,4},{24,8},{28,12},{1,17},{... | collective-permute-start | bytes 442376 | tf_op jit(solution)/shard_map/ppermute | solution.py:64
  46.0 18.7 %collective-permute-start.30 = (bf16[2,256,512]{2,1,0:T(8,128)(2,1)S(1)}, bf16[2,256,512]{2,1,0:T(8,128)(2,1)S(1)}, u32[]{:S(2)}, u32[]{:S(2)}) collective-permute-start(bf16[2,256,512]{2,1,0:T(8,128)(2,1)S(1)} %pad_maximum_fusion.refs_0_), channel_id=1, source_target_pairs={{0,1},{1,0},{2,3},{3,2},{4,5},{5,4},{6,7},{7,6},{8,9},{9,8},{10,11... | collective-permute-start | bytes 1572872 | tf_op jit(solution)/shard_map/ppermute | solution.py:261
  63.9 52.0 %collective-permute-start.28 = (bf16[1024,512]{1,0:T(8,128)(2,1)}, bf16[1024,512]{1,0:T(8,128)(2,1)S(1)}, u32[]{:S(2)}, u32[]{:S(2)}) collective-permute-start(bf16[1024,512]{1,0:T(8,128)(2,1)} %get-tuple-element.60.own_grad), channel_id=1, source_target_pairs={{0,4},{4,0},{8,12},{12,8},{16,20},{20,16},{24,28},{28,24},{1,5},{5... | collective-permute-start | bytes 3145736 | tf_op jit(solution)/shard_map/ppermute | solution.py:294
  64.7 33.8 %collective-permute-start.33 = (bf16[2,256,512]{2,1,0:T(8,128)(2,1)S(1)}, bf16[2,256,512]{2,1,0:T(8,128)(2,1)}, u32[]{:S(2)}, u32[]{:S(2)}) collective-permute-start(bf16[2,256,512]{2,1,0:T(8,128)(2,1)S(1)} %collective-permute-done.30.refs_1_), channel_id=1, source_target_pairs={{0,4},{1,2},{2,1},{3,7},{4,0},{5,6},{6,5},{7,3},{8,12},{9,10},{10,... | collective-permute-start | bytes 1572872 | tf_op jit(solution)/shard_map/ppermute | solution.py:264
  74.4 24.3 %collective-permute-start.48 = (bf16[2,128,512]{2,1,0:T(8,128)(2,1)S(1)}, bf16[2,128,512]{2,1,0:T(8,128)(2,1)S(1)}, u32[]{:S(2)}, u32[]{:S(2)}) collective-permute-start(bf16[2,128,512]{2,1,0:T(8,128)(2,1)S(1)} %pad_maximum_fusion.2.refs_0_), channel_id=1, source_target_pairs={{0,1},{1,0},{2,3},{3,2},{4,5},{5,4},{6,7},{7,6},{8,9},{9,8},{10,11... | collective-permute-start | bytes 786440 | tf_op jit(solution)/shard_map/ppermute | solution.py:261
  76.1 22.5 %collective-permute-start.49 = (bf16[2,128,512]{2,1,0:T(8,128)(2,1)S(1)}, bf16[2,128,512]{2,1,0:T(8,128)(2,1)S(1)}, u32[]{:S(2)}, u32[]{:S(2)}) collective-permute-start(bf16[2,128,512]{2,1,0:T(8,128)(2,1)S(1)} %pad_maximum_fusion.2.refs_0_), channel_id=1, source_target_pairs={{0,4},{1,2},{2,1},{3,7},{4,0},{5,6},{6,5},{7,3},{8,12},{9,10},{10,... | collective-permute-start | bytes 786440 | tf_op jit(solution)/shard_map/ppermute | solution.py:262
  76.1 39.7 %collective-permute-start.32 = (bf16[2,256,512]{2,1,0:T(8,128)(2,1)}, bf16[2,256,512]{2,1,0:T(8,128)(2,1)}, u32[]{:S(2)}, u32[]{:S(2)}) collective-permute-start(bf16[2,256,512]{2,1,0:T(8,128)(2,1)} %collective-permute-done.31.refs_4_), channel_id=1, source_target_pairs={{0,1},{1,0},{2,3},{3,2},{4,5},{5,4},{6,7},{7,6},{8,9},{9,8},{10,11... | collective-permute-start | bytes 1572872 | tf_op jit(solution)/shard_map/ppermute | solution.py:263
  98.5 24.3 %collective-permute-start.34 = (bf16[2,256,512]{2,1,0:T(8,128)(2,1)}, bf16[2,256,512]{2,1,0:T(8,128)(2,1)}, u32[]{:S(2)}, u32[]{:S(2)}) collective-permute-start(bf16[2,256,512]{2,1,0:T(8,128)(2,1)} %collective-permute-done.33.refs_5_), channel_id=1, source_target_pairs={{0,1},{1,0},{2,3},{3,2},{4,5},{5,4},{6,7},{7,6},{8,9},{9,8},{10,11... | collective-permute-start | bytes 1572872 | tf_op jit(solution)/shard_map/ppermute | solution.py:265
  100.5 30.1 %collective-permute-start.41 = (bf16[2,128,512]{2,1,0:T(8,128)(2,1)}, bf16[2,128,512]{2,1,0:T(8,128)(2,1)S(1)}, u32[]{:S(2)}, u32[]{:S(2)}) collective-permute-start(bf16[2,128,512]{2,1,0:T(8,128)(2,1)} %copy-done.13), channel_id=1, source_target_pairs={{0,1},{1,0},{2,3},{3,2},{4,5},{5,4},{6,7},{7,6},{8,9},{9,8},{10,11... | collective-permute-start | bytes 786440 | tf_op jit(solution)/shard_map/ppermute | solution.py:263
  111.7 22.3 %collective-permute-start.43 = (bf16[2,128,512]{2,1,0:T(8,128)(2,1)}, bf16[2,128,512]{2,1,0:T(8,128)(2,1)S(1)}, u32[]{:S(2)}, u32[]{:S(2)}) collective-permute-start(bf16[2,128,512]{2,1,0:T(8,128)(2,1)} %collective-permute-done.42.refs_5_), channel_id=1, source_target_pairs={{0,1},{1,0},{2,3},{3,2},{4,5},{5,4},{6,7},{7,6},{8,9},{9,8},{10,11... | collective-permute-start | bytes 786440 | tf_op jit(solution)/shard_map/ppermute | solution.py:265
  115.8 23.0 %collective-permute-start.23 = (bf16[144,512]{1,0:T(8,128)(2,1)}, bf16[144,512]{1,0:T(8,128)(2,1)S(1)}, u32[]{:S(2)}, u32[]{:S(2)}) collective-permute-start(bf16[144,512]{1,0:T(8,128)(2,1)} %copy-done.21), channel_id=1, source_target_pairs={{0,12},{4,8},{8,4},{12,0},{16,28},{20,24},{24,20},{28,16},{1,13},{... | collective-permute-start | bytes 442376 | tf_op jit(solution)/shard_map/ppermute | solution.py:64
  115.9 24.5 %collective-permute-start.50 = (bf16[2,128,512]{2,1,0:T(8,128)(2,1)}, bf16[2,128,512]{2,1,0:T(8,128)(2,1)S(1)}, u32[]{:S(2)}, u32[]{:S(2)}) collective-permute-start(bf16[2,128,512]{2,1,0:T(8,128)(2,1)} %copy-done.11), channel_id=1, source_target_pairs={{0,1},{1,0},{2,3},{3,2},{4,5},{5,4},{6,7},{7,6},{8,9},{9,8},{10,11... | collective-permute-start | bytes 786440 | tf_op jit(solution)/shard_map/ppermute | solution.py:263
  122.9 20.5 %collective-permute-start.52 = (bf16[2,128,512]{2,1,0:T(8,128)(2,1)}, bf16[2,128,512]{2,1,0:T(8,128)(2,1)S(1)}, u32[]{:S(2)}, u32[]{:S(2)}) collective-permute-start(bf16[2,128,512]{2,1,0:T(8,128)(2,1)} %collective-permute-done.51.refs_5_), channel_id=1, source_target_pairs={{0,1},{1,0},{2,3},{3,2},{4,5},{5,4},{6,7},{7,6},{8,9},{9,8},{10,11... | collective-permute-start | bytes 786440 | tf_op jit(solution)/shard_map/ppermute | solution.py:265
  130.6 26.2 %collective-permute-start.35 = (bf16[2,256,512]{2,1,0:T(8,128)(2,1)S(1)}, bf16[2,256,512]{2,1,0:T(8,128)(2,1)S(1)}, u32[]{:S(2)}, u32[]{:S(2)}) collective-permute-start(bf16[2,256,512]{2,1,0:T(8,128)(2,1)S(1)} %get-tuple-element.104), channel_id=1, source_target_pairs={{0,8},{4,12},{8,0},{12,4},{16,24},{20,28},{24,16},{28,20},{1,9},{5... | collective-permute-start | bytes 1572872 | tf_op jit(solution)/shard_map/ppermute | solution.py:317
  134.0 22.9 %collective-permute-start.36 = (bf16[2,256,512]{2,1,0:T(8,128)(2,1)S(1)}, bf16[2,256,512]{2,1,0:T(8,128)(2,1)S(1)}, u32[]{:S(2)}, u32[]{:S(2)}) collective-permute-start(bf16[2,256,512]{2,1,0:T(8,128)(2,1)S(1)} %get-tuple-element.105), channel_id=1, source_target_pairs={{0,16},{4,20},{8,24},{12,28},{16,0},{20,4},{24,8},{28,12},{1,17},{... | collective-permute-start | bytes 1572872 | tf_op jit(solution)/shard_map/ppermute | solution.py:318
  138.9 16.2 %collective-permute-start.44 = (bf16[2,128,512]{2,1,0:T(8,128)(2,1)S(1)}, bf16[2,128,512]{2,1,0:T(8,128)(2,1)S(1)}, u32[]{:S(2)}, u32[]{:S(2)}) collective-permute-start(bf16[2,128,512]{2,1,0:T(8,128)(2,1)S(1)} %get-tuple-element.111), channel_id=1, source_target_pairs={{0,8},{4,12},{8,0},{12,4},{16,24},{20,28},{24,16},{28,20},{1,9},{5... | collective-permute-start | bytes 786440 | tf_op jit(solution)/shard_map/ppermute | solution.py:317
  140.4 16.4 %collective-permute-start.45 = (bf16[2,128,512]{2,1,0:T(8,128)(2,1)S(1)}, bf16[2,128,512]{2,1,0:T(8,128)(2,1)S(1)}, u32[]{:S(2)}, u32[]{:S(2)}) collective-permute-start(bf16[2,128,512]{2,1,0:T(8,128)(2,1)S(1)} %get-tuple-element.112), channel_id=1, source_target_pairs={{0,16},{4,20},{8,24},{12,28},{16,0},{20,4},{24,8},{28,12},{1,17},{... | collective-permute-start | bytes 786440 | tf_op jit(solution)/shard_map/ppermute | solution.py:318
  153.2 17.2 %collective-permute-start.53 = (bf16[2,128,512]{2,1,0:T(8,128)(2,1)S(1)}, bf16[2,128,512]{2,1,0:T(8,128)(2,1)S(1)}, u32[]{:S(2)}, u32[]{:S(2)}) collective-permute-start(bf16[2,128,512]{2,1,0:T(8,128)(2,1)S(1)} %get-tuple-element.118), channel_id=1, source_target_pairs={{0,8},{4,12},{8,0},{12,4},{16,24},{20,28},{24,16},{28,20},{1,9},{5... | collective-permute-start | bytes 786440 | tf_op jit(solution)/shard_map/ppermute | solution.py:317
  155.1 16.9 %collective-permute-start.54 = (bf16[2,128,512]{2,1,0:T(8,128)(2,1)S(1)}, bf16[2,128,512]{2,1,0:T(8,128)(2,1)S(1)}, u32[]{:S(2)}, u32[]{:S(2)}) collective-permute-start(bf16[2,128,512]{2,1,0:T(8,128)(2,1)S(1)} %get-tuple-element.119), channel_id=1, source_target_pairs={{0,16},{4,20},{8,24},{12,28},{16,0},{20,4},{24,8},{28,12},{1,17},{... | collective-permute-start | bytes 786440 | tf_op jit(solution)/shard_map/ppermute | solution.py:318
  156.8 15.9 %collective-permute-start.26 = (bf16[144,512]{1,0:T(8,128)(2,1)S(1)}, bf16[144,512]{1,0:T(8,128)(2,1)S(1)}, u32[]{:S(2)}, u32[]{:S(2)}) collective-permute-start(bf16[144,512]{1,0:T(8,128)(2,1)S(1)} %copy-done.16), channel_id=1, source_target_pairs={{0,24},{4,28},{8,16},{12,20},{16,8},{20,12},{24,0},{28,4},{1,25},{... | collective-permute-start | bytes 442376 | tf_op jit(solution)/shard_map/ppermute | solution.py:64
  156.9 17.7 %collective-permute-start.27 = (bf16[144,512]{1,0:T(8,128)(2,1)S(1)}, bf16[144,512]{1,0:T(8,128)(2,1)S(1)}, u32[]{:S(2)}, u32[]{:S(2)}) collective-permute-start(bf16[144,512]{1,0:T(8,128)(2,1)S(1)} %get-tuple-element.99), channel_id=1, source_target_pairs={{0,28},{4,24},{8,20},{12,16},{16,12},{20,8},{24,4},{28,0},{1,29},{... | collective-permute-start | bytes 442376 | tf_op jit(solution)/shard_map/ppermute | solution.py:64
  170.5 15.6 %collective-permute-start.37 = (bf16[256,512]{1,0:T(8,128)(2,1)S(1)}, bf16[256,512]{1,0:T(8,128)(2,1)S(1)}, u32[]{:S(2)}, u32[]{:S(2)}) collective-permute-start(bf16[256,512]{1,0:T(8,128)(2,1)S(1)} %get-tuple-element.108), channel_id=1, source_target_pairs={{0,16},{4,20},{8,24},{12,28},{16,0},{20,4},{24,8},{28,12},{1,17},{... | collective-permute-start | bytes 786440 | tf_op jit(solution)/shard_map/ppermute | solution.py:332
  171.9 14.1 %collective-permute-start.38 = (bf16[256,512]{1,0:T(8,128)(2,1)S(1)}, bf16[256,512]{1,0:T(8,128)(2,1)S(1)}, u32[]{:S(2)}, u32[]{:S(2)}) collective-permute-start(bf16[256,512]{1,0:T(8,128)(2,1)S(1)} %get-tuple-element.109), channel_id=1, source_target_pairs={{0,8},{4,12},{8,0},{12,4},{16,24},{20,28},{24,16},{28,20},{1,9},{5... | collective-permute-start | bytes 786440 | tf_op jit(solution)/shard_map/ppermute | solution.py:333
  (55 other events, 715.5 us)
where the time goes:
time: 189 us; the launch traced here: 188 us
  starting transfers between devices  91.7 us (49%)
  waiting for transfers between devices  49.8 us (26%)
  Pallas kernels  34 us (18%)
  local copies, waits for them, and re-layouts  11.4 us (6%)
    pallas_call x13, Pallas kernels, run_kernel(): pl.pallas_call(body, out_shape=tuple(outs) if many else outs[0], in_specs...  34 us
    ppermute x3, starting transfers between devices, gather_planes(): a2 = lax.ppermute(b1, 'chan', outer)  33.7 us
    ppermute x28, starting transfers between devices, exchange_slots(): got.append(lax.ppermute(pieces[k], axis, pairs))  30.3 us
    ppermute x28, waiting for transfers between devices, exchange_slots(): got.append(lax.ppermute(pieces[k], axis, pairs))  23.4 us
    ppermute x3, waiting for transfers between devices, gather_planes(): a3 = lax.ppermute(b2, 'chan', outer)  11 us
    unnamed x44, local copies, waits for them, and re-layouts  7.57 us
    ppermute x3, waiting for transfers between devices, weight_finish(): last_q = lax.ppermute(next_q, 'seq', along)  6.61 us
    ppermute x3, waiting for transfers between devices, gather_planes(): a1 = lax.ppermute(block, 'chan', outer)  6.32 us
  transfers between devices with their start and end apart: 57, of which 15 were waited for; matrix products, arithmetic and copies ran while one was open for 1% of the time, Pallas kernels for 17%

commit v1 on v0

--- a/solution.py
+++ b/solution.py
@@ -11,16 +11,12 @@
 
 F32 = jnp.float32
 BF16 = jnp.bfloat16
-EXTRA = 16
-SHARES = (2, 4, 4)
+EXTRA = 8
+QUARTERS = 4
 
 
 def vmem():
     return pl.BlockSpec(memory_space=pltpu.VMEM)
-
-
-def smem():
-    return pl.BlockSpec(memory_space=pltpu.SMEM)
 
 
 def call(body, outs, scratch, flops, moved, limit_mib, *args):
@@ -29,7 +25,7 @@
 
 
 def run_kernel(body, outs, scratch, flops, moved, limit_mib, many, *args):
-    specs = [smem()] + [vmem()] * (len(args) - 1)
+    specs = [vmem()] * len(args)
     got = pl.pallas_call(
         body,
         out_shape=tuple(outs) if many else outs[0],
@@ -65,8 +61,8 @@
     return got
 
 
-def mixed_body(count, piece, group, ids, key, value, taps, *outs):
-    me = ids[0]
+def mixed_body(count, piece, group, key, value, taps, *outs):
+    me = lax.axis_index("seq")
     for k in range(count):
         dest = me ^ k
         rows = pl.ds(pl.multiple_of(dest * piece, piece), piece)
@@ -75,16 +71,16 @@
         outs[k][piece : piece + EXTRA, :] = jnp.broadcast_to(row, (EXTRA, row.shape[1])).astype(BF16)
 
 
-def upstream_body(count, piece, ids, grad, query, *outs):
-    me = ids[0]
+def upstream_body(count, piece, grad, query, *outs):
+    me = lax.axis_index("seq")
     for k in range(count):
         dest = me ^ k
         rows = pl.ds(pl.multiple_of(dest * piece, piece), piece)
         outs[k][...] = (grad[rows, :].astype(F32) * query[rows, :].astype(F32)).astype(BF16)
 
 
-def conv_body(count, piece, ids, *refs):
-    me = ids[0]
+def conv_body(count, piece, *refs):
+    me = lax.axis_index("seq")
     slots = refs[:count]
     outs = refs[count : 2 * count]
     toep = refs[2 * count]
@@ -115,8 +111,8 @@
         outs[k][...] = acc[pl.ds(pl.multiple_of(pos * piece, piece), piece), :].astype(BF16)
 
 
-def back_body(count, piece, ids, *refs):
-    me = ids[0]
+def back_body(count, piece, *refs):
+    me = lax.axis_index("seq")
     ups = refs[:count]
     slots = refs[count : 2 * count]
     toep = refs[2 * count]
@@ -135,6 +131,7 @@
     row_id = lax.broadcasted_iota(jnp.int32, (block, block), 0)
     col_id = lax.broadcasted_iota(jnp.int32, (block, block), 1)
     keep = col_id + row_id >= block - 1
+    top = lax.broadcasted_iota(jnp.int32, (EXTRA, block), 0) < EXTRA // 2
     flip = (col_id + row_id == block - 1).astype(BF16)
     turned_in = dot_nt(flip, in_all[...]).astype(BF16)
     before[...] = jnp.zeros_like(before)
@@ -151,12 +148,12 @@
         outs[k][0:piece, :] = acc[pl.ds(pl.multiple_of(pos * piece, piece), piece), :].astype(BF16)
         full = sums[pos]
         high = full.astype(BF16)
-        low = (full - high.astype(F32)).astype(BF16)
-        outs[k][piece : piece + EXTRA, :] = jnp.concatenate([high, low], axis=0)
-
-
-def query_body(count, piece, ids, *refs):
-    me = ids[0]
+        low = full - high.astype(F32)
+        outs[k][piece : piece + EXTRA, :] = jnp.where(top, high.astype(F32), low).astype(BF16)
+
+
+def query_body(count, piece, *refs):
+    me = lax.axis_index("seq")
     slots = refs[:count]
     query, grad, mixed, grad_query = refs[count:]
     for k in range(count):
@@ -167,8 +164,8 @@
         grad_query[rows, :] = (grad[rows, :].astype(F32) * conv).astype(BF16)
 
 
-def key_body(count, piece, group, factor, ids, *refs):
-    me = ids[0]
+def key_body(count, piece, group, factor, *refs):
+    me = lax.axis_index("seq")
     slots = refs[:count]
     key, value, grad_key, grad_value, taps_grad = refs[count:]
     row_id = lax.broadcasted_iota(jnp.int32, taps_grad.shape, 0)
@@ -180,58 +177,67 @@
         grad_key[rows, :] = (back * value[rows, :].astype(F32)).astype(BF16)
         grad_value[rows, :] = (back * key[rows, :].astype(F32)).astype(BF16)
         tail = slots[k][piece : piece + EXTRA, :].astype(F32)
-        row = tail[0:1, :] + tail[8:9, :]
+        row = tail[0:1, :] + tail[EXTRA // 2 : EXTRA // 2 + 1, :]
         total = total + jnp.where(row_id == pos * piece // group, row, 0.0)
     taps_grad[...] = total * factor
 
 
-def weight_body(chans, ids, own_grad, other_grad, *refs):
-    chip, plane = ids[0], ids[1]
+def stack_body(block, other, *outs):
+    rows = outs[0].shape[2]
+    first = (lax.axis_index("seq") & 1) * block.shape[0] // 2
+    for n in range(QUARTERS):
+        here = pl.ds(pl.multiple_of(first + n * rows, rows), rows)
+        out = outs[n // 2]
+        out[n % 2, 0] = block[here, :]
+        out[n % 2, 1] = other[here, :]
+
+
+def weight_body(chans, start, last, own_grad, other_grad, *refs):
+    chip, plane = lax.axis_index("seq") >> 1, lax.axis_index("chan")
     own, a1, a2, a3, b1, b2 = refs[:6]
     mine, send_p, send_q, keep_p, keep_q, stack = refs[6:]
-    rows = own.shape[1]
+    rows = mine.shape[0]
+    unit = own.shape[2]
     half = mine.shape[1] // 2
     inner = (plane == 1) | (plane == 2)
     outer = jnp.logical_not(inner)
     for r in range(chans):
         apart = (chip ^ r) ^ plane
         choices = (
-            (own, apart == 0),
-            (a1, apart == 1),
-            (b2, (apart == 2) & inner),
-            (a2, (apart == 2) & outer),
-            (b1, (apart == 3) & inner),
-            (a3, (apart == 3) & outer),
+            (own, 0, apart == 0),
+            (a1, 0, apart == 1),
+            (b2, 0, (apart == 2) & inner),
+            (a2, 0, (apart == 2) & outer),
+            (b1, 0, (apart == 3) & inner),
+            (a3, last, (apart == 3) & outer),
         )
-        for source, chosen in choices:
+        for source, offset, chosen in choices:
 
             @pl.when(chosen)
-            def _(source=source, r=r):
-                stack[0, r * rows : (r + 1) * rows, :] = source[0]
-                stack[1, r * rows : (r + 1) * rows, :] = source[1]
-
-    def part(r, first):
-        a = stack[0, r * rows : (r + 1) * rows, :]
-        b = stack[1, r * rows : (r + 1) * rows, :]
-        cols = slice(first, first + half)
-        return dot_nt(a, own_grad[cols, :]) + dot_nt(b, other_grad[cols, :])
+            def _(source=source, offset=offset, r=r):
+                for n in range(rows // unit):
+                    at = r * rows + n * unit
+                    for side in range(2):
+                        stack[side, at : at + unit, :] = source[start + n - offset, side]
 
     for side in range(2):
-        first = side * half
-        send = (send_p, send_q)[side]
-        order = (1, 3) if side == 0 else (2, 3)
-        for n in range(2):
-            send[n] = part(order[n], first).astype(BF16)
-        (keep_p, keep_q)[side][...] = part(3 - order[0], first)
-        mine[:, first : first + half] = part(0, first)
-
-
-def middle_body(ids, keep_p, got_p, keep_q, got_q, out_p, out_q):
+        cols = slice(side * half, (side + 1) * half)
+        full = dot_nt(stack[0], own_grad[cols, :]) + dot_nt(stack[1], other_grad[cols, :])
+        parts = [full[r * rows : (r + 1) * rows, :] for r in range(chans)]
+        given = (send_p, send_q)[side]
+        near = 1 + side
+        given[0] = parts[near].astype(BF16)
+        given[1] = parts[3].astype(BF16)
+        (keep_p, keep_q)[side][...] = parts[3 - near]
+        mine[:, cols] = parts[0]
+
+
+def middle_body(keep_p, got_p, keep_q, got_q, out_p, out_q):
     out_p[...] = (keep_p[...] + got_p[1].astype(F32)).astype(BF16)
     out_q[...] = (keep_q[...] + got_q[1].astype(F32)).astype(BF16)
 
 
-def finish_body(chunks, factor, ids, *refs):
+def finish_body(chunks, factor, *refs):
     out = refs[-1]
     half = refs[0].shape[1] // 2
     first = 0
@@ -255,36 +261,38 @@
     return outer, middle
 
 
-def gather_planes(block, seqs, chans):
+def weight_start(layer_input):
+    channels, tok = layer_input.shape
+    seqs, chans = lax.axis_size("seq"), lax.axis_size("chan")
+    half = channels // 2
+    swap = [(i, i ^ 1) for i in range(seqs)]
+    other = lax.ppermute(layer_input, "seq", swap)
+    quarter = struct((QUARTERS // 2, 2, half // QUARTERS, tok), BF16)
+    own = call(
+        stack_body, [quarter] * 2, [], half * tok, 4 * half * tok, 58,
+        layer_input, other,
+    )
     outer, middle = plane_pairs(seqs, chans)
     both = ("seq", "chan")
-    a1 = lax.ppermute(block, "chan", outer)
-    b1 = lax.ppermute(block, both, middle)
-    a2 = lax.ppermute(b1, "chan", outer)
-    b2 = lax.ppermute(a1, both, middle)
-    a3 = lax.ppermute(b2, "chan", outer)
-    return [block, a1, a2, a3, b1, b2]
-
-
-def weight_start(layer_input, seq_id):
-    channels, _ = layer_input.shape
-    seqs, chans = lax.axis_size("seq"), lax.axis_size("chan")
-    half = channels // 2
-    core = seq_id & 1
-    swap = [(i, i ^ 1) for i in range(seqs)]
-    give = lax.dynamic_slice_in_dim(layer_input, (1 - core) * half, half, 0)
-    keep = lax.dynamic_slice_in_dim(layer_input, core * half, half, 0)
-    other = lax.ppermute(give, "seq", swap)
-    gathered = []
-    first = 0
-    for share in SHARES:
-        here = slice(first, first + half // share)
-        first += half // share
-        gathered.append(gather_planes(jnp.stack([keep[here], other[here]]), seqs, chans))
-    return gathered
-
-
-def weight_finish(gathered, grad_query, seq_id, chan_id, factor):
+    a1x = lax.ppermute(own[0], "chan", outer)
+    b1x = lax.ppermute(own[0], both, middle)
+    a1y = lax.ppermute(own[1], "chan", outer)
+    b1y = lax.ppermute(own[1], both, middle)
+    a2x = lax.ppermute(b1x, "chan", outer)
+    b2x = lax.ppermute(a1x, both, middle)
+    a3x = lax.ppermute(b2x, "chan", outer)
+    a2y = lax.ppermute(b1y, "chan", outer)
+    b2y = lax.ppermute(a1y, both, middle)
+    a3y = lax.ppermute(b2y[0:1], "chan", outer)
+    a3z = lax.ppermute(b2y[1:2], "chan", outer)
+    return [
+        (0, 2, 0, (own[0], a1x, a2x, a3x, b1x, b2x)),
+        (0, 1, 0, (own[1], a1y, a2y, a3y, b1y, b2y)),
+        (1, 1, 1, (own[1], a1y, a2y, a3z, b1y, b2y)),
+    ]
+
+
+def weight_finish(gathered, grad_query, factor):
     seqs, chans = lax.axis_size("seq"), lax.axis_size("chan")
     outputs, tok = grad_query.shape
     half = outputs // 2
@@ -292,12 +300,11 @@
     along = [(i, i ^ 2) for i in range(seqs)]
     across = [(i, i ^ 4) for i in range(seqs)]
     other_grad = lax.ppermute(grad_query, "seq", swap)
-    ids = jnp.stack([seq_id >> 1, chan_id])
     parts = []
-    for sources in gathered:
-        rows = sources[0].shape[1]
+    for start, count, last, sources in gathered:
+        rows = count * sources[0].shape[2]
         mine, send_p, send_q, keep_p, keep_q = call(
-            functools.partial(weight_body, chans),
+            functools.partial(weight_body, chans, start, last),
             [
                 struct((rows, outputs), F32),
                 struct((2, rows, half), BF16),
@@ -309,7 +316,6 @@
             4 * chans * rows * outputs * tok,
             12 << 20,
             20,
-            ids,
             grad_query,
             other_grad,
             *sources,
@@ -323,7 +329,6 @@
             rows * outputs,
             4 << 20,
             8,
-            ids,
             keep_p,
             got_p,
             keep_q,
@@ -334,19 +339,14 @@
         parts += [mine, got_p, got_q, last_p, last_q]
     (out,) = call(
         functools.partial(finish_body, len(gathered), factor),
-        [struct((channels_of(gathered), outputs), F32)],
+        [struct((QUARTERS * gathered[0][3][0].shape[2], outputs), F32)],
         [],
         3 * outputs * outputs,
         8 << 20,
         16,
-        ids,
         *parts,
     )
     return out
-
-
-def channels_of(gathered):
-    return sum(sources[0].shape[1] for sources in gathered)
 
 
 def weight_general(layer_input, grad_query, factor):
@@ -369,9 +369,6 @@
     group = channels // filter_taps.shape[0]
     weight_factor = 1.0 / math.sqrt(length)
     taps_factor = 1.0 / math.sqrt(group * length)
-    seq_id = lax.axis_index("seq")
-    chan_id = lax.axis_index("chan")
-    ids = jnp.stack([seq_id, chan_id])
     special = seqs == 8 and chans == 4
     small = struct((piece, tok), BF16)
     large = struct((piece + EXTRA, tok), BF16)
@@ -384,47 +381,47 @@
 
     mixed = call(
         functools.partial(mixed_body, seqs, piece, group),
-        [large] * seqs, [], 3 * unit, 6 * unit, 16,
-        ids, key_proj, value_proj, filter_taps,
+        [large] * seqs, [], 3 * unit, 6 * unit, 58,
+        key_proj, value_proj, filter_taps,
     )
     mixed_slots = exchange_slots(mixed, "seq")
     upstream = call(
         functools.partial(upstream_body, seqs, piece),
         [small] * seqs, [], 3 * unit, 6 * unit, 16,
-        ids, grad_out, query_proj,
+        grad_out, query_proj,
     )
     up_slots = exchange_slots(upstream, "seq")
     if special:
-        gathered = weight_start(layer_input, seq_id)
+        gathered = weight_start(layer_input)
     conv = call(
         functools.partial(conv_body, seqs, piece),
         [small] * seqs + [struct((seqs, tok, tok), BF16)],
         [flat, rows8, wide, square],
         work, 16 * unit, 22,
-        ids, *mixed_slots,
+        *mixed_slots,
     )
     conv_slots = exchange_slots(conv[:seqs], "seq")
     mixed_out, grad_query = call(
         functools.partial(query_body, seqs, piece),
         [struct((channels, tok), BF16)] * 2, [], 4 * unit, 10 * unit, 16,
-        ids, *conv_slots, query_proj, grad_out,
+        *conv_slots, query_proj, grad_out,
     )
     back = call(
         functools.partial(back_body, seqs, piece),
         [large] * seqs,
         [flat, flat, wide, square, rows8],
         2 * work, 20 * unit, 24,
-        ids, *up_slots, *mixed_slots, conv[seqs],
+        *up_slots, *mixed_slots, conv[seqs],
     )
     back_slots = exchange_slots(back, "seq")
     grad_key, grad_value, filter_grad = call(
         functools.partial(key_body, seqs, piece, group, taps_factor),
         [struct((channels, tok), BF16)] * 2 + [struct(filter_taps.shape, F32)],
         [], 4 * unit, 10 * unit, 16,
-        ids, *back_slots, key_proj, value_proj,
+        *back_slots, key_proj, value_proj,
     )
     if special:
-        weight_grad = weight_finish(gathered, grad_query, seq_id, chan_id, weight_factor)
+        weight_grad = weight_finish(gathered, grad_query, weight_factor)
     else:
         weight_grad = weight_general(layer_input, grad_query, weight_factor)
     return (mixed_out, grad_query, grad_key, grad_value, filter_grad, weight_grad)

time: 189 us -> 166 us (0.88)
  starting transfers between devices: 91.7 us -> 82.8 us
  Pallas kernels: 34 us -> 26.9 us
  local copies, waits for them, and re-layouts: 11.4 us -> 4.38 us
    ppermute x28, waiting for transfers between devices: 23.4 us -> 37.6 us  [exchange_slots(): got.append(lax.ppermute(pieces[k], axis, pairs))]
    ppermute x16 -> x12, waiting for transfers between devices: 18 us -> 4.01 us  [the longest x1 3.98 us: weight_start(): a3y = lax.ppermute(b2y[0:1], 'chan', outer)]
    ppermute x16 -> x12, starting transfers between devices: 47.5 us -> 40.1 us  [the longest x1 13.3 us: weight_start(): a2x = lax.ppermute(b1x, 'chan', outer)]
    pallas_call x13 -> x14, Pallas kernels: 34 us -> 26.9 us  [run_kernel(): pl.pallas_call(body, out_shape=tuple(outs) if many else outs[0], in_specs...]
    unnamed x44 -> x24, local copies, waits for them, and re-layouts: 7.57 us -> 4.35 us
    ppermute x3, waiting for transfers between devices: 6.61 us -> 8.86 us  [weight_finish(): last_q = lax.ppermute(next_q, 'seq', along)]
    another operation x4 -> x0, local copies, waits for them, and re-layouts: 1.99 us -> none  [weight_start(): jnp.stack([keep[here], other[here]])]
  transfers between devices with their start and end apart: 57 -> 53, of which waited for: 15 -> 14; matrix products, arithmetic and copies ran while one was open for 1% -> 0% of each run, Pallas kernels for 17% -> 15%
where the time goes in v1:
time: 166 us
  starting transfers between devices  82.8 us (50%)
  waiting for transfers between devices  50.7 us (31%)
  Pallas kernels  26.9 us (16%)
  local copies, waits for them, and re-layouts  4.38 us (3%)
    ppermute x28, waiting for transfers between devices, exchange_slots(): got.append(lax.ppermute(pieces[k], axis, pairs))  37.6 us
    ppermute x28, starting transfers between devices, exchange_slots(): got.append(lax.ppermute(pieces[k], axis, pairs))  29.8 us
    pallas_call x14, Pallas kernels, run_kernel(): pl.pallas_call(body, out_shape=tuple(outs) if many else outs[0], in_specs...  26.9 us
    ppermute x1, starting transfers between devices, weight_start(): a2x = lax.ppermute(b1x, 'chan', outer)  13.3 us
    ppermute x1, starting transfers between devices, weight_start(): a3x = lax.ppermute(b2x, 'chan', outer)  11.2 us
    ppermute x1, starting transfers between devices, weight_start(): a2y = lax.ppermute(b1y, 'chan', outer)  10.2 us
    ppermute x3, waiting for transfers between devices, weight_finish(): last_q = lax.ppermute(next_q, 'seq', along)  8.86 us
    ppermute x3, starting transfers between devices, weight_finish(): got_p = lax.ppermute(send_p, 'seq', along)  4.92 us
  transfers between devices with their start and end apart: 53, of which 14 were waited for; matrix products, arithmetic and copies ran while one was open for 0% of the time, Pallas kernels for 15%

profile of v1, /device:TPU:0, one launch (start us, length us, event | category | flops | bytes accessed | tf_op | source)
XLA Modules:
  0.0 165.7 jit_solution(7906227563774557765)
XLA Ops:
  4.0 2.7 %shard_map.109 = (bf16[136,512]{1,0:T(8,128)(2,1)}, bf16[136,512]{1,0:T(8,128)(2,1)}, bf16[136,512]{1,0:T(8,128)(2,1)}, bf16[136,512]{1,0:T(8,128)(2,1)}, bf16[1...) custom-call(bf16[1024,512]{1,0:T(8,128)(2,1)} %refs_8_.3, ...), custom_call_target="tpu_custom_call" | custom-call | flops 1572864 | bytes 3145728 | tf_op jit(solution)/shard_map/pallas_call | solution.py:29
  7.2 2.5 %collective-permute-start.1 = (bf16[136,512]{1,0:T(8,128)(2,1)}, bf16[136,512]{1,0:T(8,128)(2,1)S(1)}, u32[]{:S(2)}, u32[]{:S(2)}) collective-permute-start(bf16[136,512]{1,0:T(8,128)(2,1)} %get-tuple-element.69), channel_id=1, source_target_pairs={{0,8},{4,12},{8,0},{12,4},{16,24},{20,28},{24,16},{28,20},{1,9},{5... | collective-permute-start | bytes 417800 | tf_op jit(solution)/shard_map/ppermute | solution.py:60
  11.5 2.9 %collective-permute-done.1.refs_2_.refs_10_ = bf16[136,512]{1,0:T(8,128)(2,1)S(1)} collective-permute-done((bf16[136,512]{1,0:T(8,128)(2,1)}, bf16[136,512]{1,0:T(8,128)(2,1)S(1)}, u32[]{:S(2)}, u32[]{:S(2)}) %collective-permute-start.1) | collective-permute-done | bytes 139296 | tf_op jit(solution)/shard_map/ppermute | solution.py:60
  14.4 3.0 %collective-permute-start.5 = (bf16[136,512]{1,0:T(8,128)(2,1)}, bf16[136,512]{1,0:T(8,128)(2,1)S(1)}, u32[]{:S(2)}, u32[]{:S(2)}) collective-permute-start(bf16[136,512]{1,0:T(8,128)(2,1)} %get-tuple-element.73), channel_id=1, source_target_pairs={{0,24},{4,28},{8,16},{12,20},{16,8},{20,12},{24,0},{28,4},{1,25},{... | collective-permute-start | bytes 417800 | tf_op jit(solution)/shard_map/ppermute | solution.py:60
  18.3 2.6 %shard_map.115 = (bf16[2,2,128,512]{3,2,1,0:T(8,128)(2,1)}, bf16[2,2,128,512]{3,2,1,0:T(8,128)(2,1)}) custom-call(bf16[1024,512]{1,0:T(8,128)(2,1)} %block.1, bf16[1024,512]{1,0:T(8,128)(2,1)} %copy-done.11), custom_call_target="tpu_custom_call" | custom-call | flops 262144 | bytes 1048576 | tf_op jit(solution)/shard_map/pallas_call | solution.py:29
  29.0 4.0 %shard_map.110 = (bf16[128,512]{1,0:T(8,128)(2,1)S(1)}, bf16[128,512]{1,0:T(8,128)(2,1)S(1)}, bf16[128,512]{1,0:T(8,128)(2,1)S(1)}, bf16[128,512]{1,0:T(8,128)(2...) custom-call(bf16[136,512]{1,0:T(8,128)(2,1)S(1)} %copy-done.9, ...), custom_call_target="tpu_custom_call" | custom-call | flops 2415919104 | bytes 8388608 | tf_op jit(solution)/shard_map/pallas_call | solution.py:29
  36.4 3.1 %collective-permute-done.8.refs_2_ = bf16[128,512]{1,0:T(8,128)(2,1)S(1)} collective-permute-done((bf16[128,512]{1,0:T(8,128)(2,1)S(1)}, bf16[128,512]{1,0:T(8,128)(2,1)S(1)}, u32[]{:S(2)}, u32[]{:S(2)}) %collective-permute-start.8) | collective-permute-done | bytes 131104 | tf_op jit(solution)/shard_map/ppermute | solution.py:60
  41.2 2.3 %collective-permute-start.12 = (bf16[128,512]{1,0:T(8,128)(2,1)S(1)}, bf16[128,512]{1,0:T(8,128)(2,1)S(1)}, u32[]{:S(2)}, u32[]{:S(2)}) collective-permute-start(bf16[128,512]{1,0:T(8,128)(2,1)S(1)} %get-tuple-element.81), channel_id=1, source_target_pairs={{0,24},{4,28},{8,16},{12,20},{16,8},{20,12},{24,0},{28,4},{1,25},{... | collective-permute-start | bytes 393224 | tf_op jit(solution)/shard_map/ppermute | solution.py:60
  45.9 2.5 %collective-permute-done.12.refs_6_ = bf16[128,512]{1,0:T(8,128)(2,1)S(1)} collective-permute-done((bf16[128,512]{1,0:T(8,128)(2,1)S(1)}, bf16[128,512]{1,0:T(8,128)(2,1)S(1)}, u32[]{:S(2)}, u32[]{:S(2)}) %collective-permute-start.12) | collective-permute-done | bytes 131104 | tf_op jit(solution)/shard_map/ppermute | solution.py:60
  50.7 2.5 %collective-permute-start.19 = (bf16[128,512]{1,0:T(8,128)(2,1)S(1)}, bf16[128,512]{1,0:T(8,128)(2,1)S(1)}, u32[]{:S(2)}, u32[]{:S(2)}) collective-permute-start(bf16[128,512]{1,0:T(8,128)(2,1)S(1)} %get-tuple-element.91), channel_id=1, source_target_pairs={{0,24},{4,28},{8,16},{12,20},{16,8},{20,12},{24,0},{28,4},{1,25},{... | collective-permute-start | bytes 393224 | tf_op jit(solution)/shard_map/ppermute | solution.py:60
  55.0 2.2 %collective-permute-done.19.refs_6_ = bf16[128,512]{1,0:T(8,128)(2,1)S(1)} collective-permute-done((bf16[128,512]{1,0:T(8,128)(2,1)S(1)}, bf16[128,512]{1,0:T(8,128)(2,1)S(1)}, u32[]{:S(2)}, u32[]{:S(2)}) %collective-permute-start.19) | collective-permute-done | bytes 131104 | tf_op jit(solution)/shard_map/ppermute | solution.py:60
  57.1 2.6 %collective-permute-start.20 = (bf16[128,512]{1,0:T(8,128)(2,1)S(1)}, bf16[128,512]{1,0:T(8,128)(2,1)S(1)}, u32[]{:S(2)}, u32[]{:S(2)}) collective-permute-start(bf16[128,512]{1,0:T(8,128)(2,1)S(1)} %get-tuple-element.92), channel_id=1, source_target_pairs={{0,28},{4,24},{8,20},{12,16},{16,12},{20,8},{24,4},{28,0},{1,29},{... | collective-permute-start | bytes 393224 | tf_op jit(solution)/shard_map/ppermute | solution.py:60
  59.7 13.3 %collective-permute-start.32 = (bf16[2,2,128,512]{3,2,1,0:T(8,128)(2,1)S(1)}, bf16[2,2,128,512]{3,2,1,0:T(8,128)(2,1)S(1)}, u32[]{:S(2)}, u32[]{:S(2)}) collective-permute-start(bf16[2,2,128,512]{3,2,1,0:T(8,128)(2,1)S(1)} %collective-permute-done.31.refs_4_), channel_id=1, source_target_pairs={{0,1},{1,0},{2,3},{3,2},{4,5},{5,4},{6,7},{7,6},{8,9},{9,8},{10,11... | collective-permute-start | bytes 1572872 | tf_op jit(solution)/shard_map/ppermute | solution.py:281
  73.0 11.2 %collective-permute-start.34 = (bf16[2,2,128,512]{3,2,1,0:T(8,128)(2,1)S(1)}, bf16[2,2,128,512]{3,2,1,0:T(8,128)(2,1)S(1)}, u32[]{:S(2)}, u32[]{:S(2)}) collective-permute-start(bf16[2,2,128,512]{3,2,1,0:T(8,128)(2,1)S(1)} %collective-permute-done.33.refs_5_), channel_id=1, source_target_pairs={{0,1},{1,0},{2,3},{3,2},{4,5},{5,4},{6,7},{7,6},{8,9},{9,8},{10,11... | collective-permute-start | bytes 1572872 | tf_op jit(solution)/shard_map/ppermute | solution.py:283
  84.3 10.2 %collective-permute-start.41 = (bf16[2,2,128,512]{3,2,1,0:T(8,128)(2,1)S(1)}, bf16[2,2,128,512]{3,2,1,0:T(8,128)(2,1)S(1)}, u32[]{:S(2)}, u32[]{:S(2)}) collective-permute-start(bf16[2,2,128,512]{3,2,1,0:T(8,128)(2,1)S(1)} %collective-permute-done.40.refs_4_), channel_id=1, source_target_pairs={{0,1},{1,0},{2,3},{3,2},{4,5},{5,4},{6,7},{7,6},{8,9},{9,8},{10,11... | collective-permute-start | bytes 1572872 | tf_op jit(solution)/shard_map/ppermute | solution.py:284
  94.6 6.4 %shard_map.113 = (bf16[136,512]{1,0:T(8,128)(2,1)S(1)}, bf16[136,512]{1,0:T(8,128)(2,1)S(1)}, bf16[136,512]{1,0:T(8,128)(2,1)S(1)}, bf16[136,512]{1,0:T(8,128)(2...) custom-call(bf16[128,512]{1,0:T(8,128)(2,1)S(1)} %get-tuple-element., ...), custom_call_target="tpu_custom_call" | custom-call | flops 4831838208 | bytes 10485760 | tf_op jit(solution)/shard_map/pallas_call | solution.py:29
  102.6 2.0 %collective-permute-start.48 = (bf16[1,2,128,512]{3,2,1,0:T(8,128)(2,1)S(1)}, bf16[1,2,128,512]{3,2,1,0:T(8,128)(2,1)S(1)}, u32[]{:S(2)}, u32[]{:S(2)}) collective-permute-start(bf16[1,2,128,512]{3,2,1,0:T(8,128)(2,1)S(1)} %get-tuple-element.128), channel_id=1, source_target_pairs={{0,1},{1,0},{2,3},{3,2},{4,5},{5,4},{6,7},{7,6},{8,9},{9,8},{10,11... | collective-permute-start | bytes 786440 | tf_op jit(solution)/shard_map/ppermute | solution.py:287
  104.6 2.8 %shard_map.116 = (f32[256,1024]{1,0:T(8,128)S(1)}, bf16[2,256,512]{2,1,0:T(8,128)(2,1)S(1)}, bf16[2,256,512]{2,1,0:T(8,128)(2,1)S(1)}, f32[256,512]{1,0:T(8,128)S(1)}, f32[256,512]{1,0:T(8,128)S(1)}) custom-call(bf16[1024,512]{1,0:T(8,128)(2,1)S(1)} %copy-done, bf16[1024,512]{1,0:T(8,128)(2,1)S(1)} %collective-permute-done.28.other_grad, ...), custom_call_target="tpu_custom_call" | custom-call | flops 2147483648 | bytes 12582912 | tf_op jit(solution)/shard_map/pallas_call | solution.py:29
  108.9 4.0 %collective-permute-done.43.refs_3_ = bf16[1,2,128,512]{3,2,1,0:T(8,128)(2,1)S(1)} collective-permute-done((bf16[1,2,128,512]{3,2,1,0:T(8,128)(2,1)S(1)}, bf16[1,2,128,512]{3,2,1,0:T(8,128)(2,1)S(1)}, u32[]{:S(2)}, u32[]{:S(2)}) %collective-permute-start.43) | collective-permute-done | bytes 262176 | tf_op jit(solution)/shard_map/ppermute | solution.py:286
  119.6 12.8 %collective-permute-done.24.refs_4_ = bf16[136,512]{1,0:T(8,128)(2,1)S(1)} collective-permute-done((bf16[136,512]{1,0:T(8,128)(2,1)S(1)}, bf16[136,512]{1,0:T(8,128)(2,1)S(1)}, u32[]{:S(2)}, u32[]{:S(2)}) %collective-permute-start.24) | collective-permute-done | bytes 139296 | tf_op jit(solution)/shard_map/ppermute | solution.py:60
  135.9 2.7 %collective-permute-start.27 = (bf16[136,512]{1,0:T(8,128)(2,1)S(1)}, bf16[136,512]{1,0:T(8,128)(2,1)S(1)}, u32[]{:S(2)}, u32[]{:S(2)}) collective-permute-start(bf16[136,512]{1,0:T(8,128)(2,1)S(1)} %get-tuple-element.101), channel_id=1, source_target_pairs={{0,28},{4,24},{8,20},{12,16},{16,12},{20,8},{24,4},{28,0},{1,29},{... | collective-permute-start | bytes 417800 | tf_op jit(solution)/shard_map/ppermute | solution.py:60
  138.8 8.6 %collective-permute-done.25.refs_5_ = bf16[136,512]{1,0:T(8,128)(2,1)S(1)} collective-permute-done((bf16[136,512]{1,0:T(8,128)(2,1)S(1)}, bf16[136,512]{1,0:T(8,128)(2,1)S(1)}, u32[]{:S(2)}, u32[]{:S(2)}) %collective-permute-start.25) | collective-permute-done | bytes 139296 | tf_op jit(solution)/shard_map/ppermute | solution.py:60
  154.9 6.3 %collective-permute-done.47.refs_9_ = bf16[128,512]{1,0:T(8,128)(2,1)S(1)} collective-permute-done((bf16[128,512]{1,0:T(8,128)(2,1)S(1)}, bf16[128,512]{1,0:T(8,128)(2,1)S(1)}, u32[]{:S(2)}, u32[]{:S(2)}) %collective-permute-start.47) | collective-permute-done | bytes 131104 | tf_op jit(solution)/shard_map/ppermute | solution.py:338
  161.4 2.6 %collective-permute-done.52.refs_14_ = bf16[128,512]{1,0:T(8,128)(2,1)S(1)} collective-permute-done((bf16[128,512]{1,0:T(8,128)(2,1)S(1)}, bf16[128,512]{1,0:T(8,128)(2,1)S(1)}, u32[]{:S(2)}, u32[]{:S(2)}) %collective-permute-start.52) | collective-permute-done | bytes 131104 | tf_op jit(solution)/shard_map/ppermute | solution.py:338
  (121 shorter events, 49.2 us)
Async XLA Ops:
  0.6 16.7 %collective-permute-start.29 = (bf16[1024,512]{1,0:T(8,128)(2,1)}, bf16[1024,512]{1,0:T(8,128)(2,1)S(1)}, u32[]{:S(2)}, u32[]{:S(2)}) collective-permute-start(bf16[1024,512]{1,0:T(8,128)(2,1)} %block.1), channel_id=1, source_target_pairs={{0,4},{4,0},{8,12},{12,8},{16,20},{20,16},{24,28},{28,24},{1,5},{5... | collective-permute-start | bytes 3145736 | tf_op jit(solution)/shard_map/ppermute | solution.py:269
  20.9 24.5 %collective-permute-start.30 = (bf16[2,2,128,512]{3,2,1,0:T(8,128)(2,1)}, bf16[2,2,128,512]{3,2,1,0:T(8,128)(2,1)S(1)}, u32[]{:S(2)}, u32[]{:S(2)}) collective-permute-start(bf16[2,2,128,512]{3,2,1,0:T(8,128)(2,1)} %get-tuple-element.105.refs_0_), channel_id=1, source_target_pairs={{0,1},{1,0},{2,3},{3,2},{4,5},{5,4},{6,7},{7,6},{8,9},{9,8},{10,11... | collective-permute-start | bytes 1572872 | tf_op jit(solution)/shard_map/ppermute | solution.py:277
  22.5 23.2 %collective-permute-start.39 = (bf16[2,2,128,512]{3,2,1,0:T(8,128)(2,1)}, bf16[2,2,128,512]{3,2,1,0:T(8,128)(2,1)S(1)}, u32[]{:S(2)}, u32[]{:S(2)}) collective-permute-start(bf16[2,2,128,512]{3,2,1,0:T(8,128)(2,1)} %get-tuple-element.113.refs_0_), channel_id=1, source_target_pairs={{0,1},{1,0},{2,3},{3,2},{4,5},{5,4},{6,7},{7,6},{8,9},{9,8},{10,11... | collective-permute-start | bytes 1572872 | tf_op jit(solution)/shard_map/ppermute | solution.py:279
  45.4 14.3 %collective-permute-start.33 = (bf16[2,2,128,512]{3,2,1,0:T(8,128)(2,1)S(1)}, bf16[2,2,128,512]{3,2,1,0:T(8,128)(2,1)S(1)}, u32[]{:S(2)}, u32[]{:S(2)}) collective-permute-start(bf16[2,2,128,512]{3,2,1,0:T(8,128)(2,1)S(1)} %collective-permute-done.30.refs_1_), channel_id=1, source_target_pairs={{0,4},{1,2},{2,1},{3,7},{4,0},{5,6},{6,5},{7,3},{8,12},{9,10},{10,... | collective-permute-start | bytes 1572872 | tf_op jit(solution)/shard_map/ppermute | solution.py:282
  45.7 27.3 %collective-permute-start.42 = (bf16[2,2,128,512]{3,2,1,0:T(8,128)(2,1)S(1)}, bf16[2,2,128,512]{3,2,1,0:T(8,128)(2,1)S(1)}, u32[]{:S(2)}, u32[]{:S(2)}) collective-permute-start(bf16[2,2,128,512]{3,2,1,0:T(8,128)(2,1)S(1)} %collective-permute-done.39.refs_1_), channel_id=1, source_target_pairs={{0,4},{1,2},{2,1},{3,7},{4,0},{5,6},{6,5},{7,3},{8,12},{9,10},{10,... | collective-permute-start | bytes 1572872 | tf_op jit(solution)/shard_map/ppermute | solution.py:285
  55.0 46.0 %collective-permute-start.28 = (bf16[1024,512]{1,0:T(8,128)(2,1)}, bf16[1024,512]{1,0:T(8,128)(2,1)S(1)}, u32[]{:S(2)}, u32[]{:S(2)}) collective-permute-start(bf16[1024,512]{1,0:T(8,128)(2,1)} %get-tuple-element.62.own_grad), channel_id=1, source_target_pairs={{0,4},{4,0},{8,12},{12,8},{16,20},{20,16},{24,28},{28,24},{1,5},{5... | collective-permute-start | bytes 3145736 | tf_op jit(solution)/shard_map/ppermute | solution.py:302
  57.1 27.2 %collective-permute-start.40 = (bf16[2,2,128,512]{3,2,1,0:T(8,128)(2,1)S(1)}, bf16[2,2,128,512]{3,2,1,0:T(8,128)(2,1)S(1)}, u32[]{:S(2)}, u32[]{:S(2)}) collective-permute-start(bf16[2,2,128,512]{3,2,1,0:T(8,128)(2,1)S(1)} %copy-done.7), channel_id=1, source_target_pairs={{0,4},{1,2},{2,1},{3,7},{4,0},{5,6},{6,5},{7,3},{8,12},{9,10},{10,... | collective-permute-start | bytes 1572872 | tf_op jit(solution)/shard_map/ppermute | solution.py:280
  57.1 37.4 %collective-permute-start.20 = (bf16[128,512]{1,0:T(8,128)(2,1)S(1)}, bf16[128,512]{1,0:T(8,128)(2,1)S(1)}, u32[]{:S(2)}, u32[]{:S(2)}) collective-permute-start(bf16[128,512]{1,0:T(8,128)(2,1)S(1)} %get-tuple-element.92), channel_id=1, source_target_pairs={{0,28},{4,24},{8,20},{12,16},{16,12},{20,8},{24,4},{28,0},{1,29},{... | collective-permute-start | bytes 393224 | tf_op jit(solution)/shard_map/ppermute | solution.py:60
  59.7 41.3 %collective-permute-start.32 = (bf16[2,2,128,512]{3,2,1,0:T(8,128)(2,1)S(1)}, bf16[2,2,128,512]{3,2,1,0:T(8,128)(2,1)S(1)}, u32[]{:S(2)}, u32[]{:S(2)}) collective-permute-start(bf16[2,2,128,512]{3,2,1,0:T(8,128)(2,1)S(1)} %collective-permute-done.31.refs_4_), channel_id=1, source_target_pairs={{0,1},{1,0},{2,3},{3,2},{4,5},{5,4},{6,7},{7,6},{8,9},{9,8},{10,11... | collective-permute-start | bytes 1572872 | tf_op jit(solution)/shard_map/ppermute | solution.py:281
  73.0 29.5 %collective-permute-start.34 = (bf16[2,2,128,512]{3,2,1,0:T(8,128)(2,1)S(1)}, bf16[2,2,128,512]{3,2,1,0:T(8,128)(2,1)S(1)}, u32[]{:S(2)}, u32[]{:S(2)}) collective-permute-start(bf16[2,2,128,512]{3,2,1,0:T(8,128)(2,1)S(1)} %collective-permute-done.33.refs_5_), channel_id=1, source_target_pairs={{0,1},{1,0},{2,3},{3,2},{4,5},{5,4},{6,7},{7,6},{8,9},{9,8},{10,11... | collective-permute-start | bytes 1572872 | tf_op jit(solution)/shard_map/ppermute | solution.py:283
  84.3 23.1 %collective-permute-start.41 = (bf16[2,2,128,512]{3,2,1,0:T(8,128)(2,1)S(1)}, bf16[2,2,128,512]{3,2,1,0:T(8,128)(2,1)S(1)}, u32[]{:S(2)}, u32[]{:S(2)}) collective-permute-start(bf16[2,2,128,512]{3,2,1,0:T(8,128)(2,1)S(1)} %collective-permute-done.40.refs_4_), channel_id=1, source_target_pairs={{0,1},{1,0},{2,3},{3,2},{4,5},{5,4},{6,7},{7,6},{8,9},{9,8},{10,11... | collective-permute-start | bytes 1572872 | tf_op jit(solution)/shard_map/ppermute | solution.py:284
  94.5 18.4 %collective-permute-start.43 = (bf16[1,2,128,512]{3,2,1,0:T(8,128)(2,1)S(1)}, bf16[1,2,128,512]{3,2,1,0:T(8,128)(2,1)S(1)}, u32[]{:S(2)}, u32[]{:S(2)}) collective-permute-start(bf16[1,2,128,512]{3,2,1,0:T(8,128)(2,1)S(1)} %get-tuple-element.129), channel_id=1, source_target_pairs={{0,1},{1,0},{2,3},{3,2},{4,5},{5,4},{6,7},{7,6},{8,9},{9,8},{10,11... | collective-permute-start | bytes 786440 | tf_op jit(solution)/shard_map/ppermute | solution.py:286
  102.6 15.4 %collective-permute-start.48 = (bf16[1,2,128,512]{3,2,1,0:T(8,128)(2,1)S(1)}, bf16[1,2,128,512]{3,2,1,0:T(8,128)(2,1)S(1)}, u32[]{:S(2)}, u32[]{:S(2)}) collective-permute-start(bf16[1,2,128,512]{3,2,1,0:T(8,128)(2,1)S(1)} %get-tuple-element.128), channel_id=1, source_target_pairs={{0,1},{1,0},{2,3},{3,2},{4,5},{5,4},{6,7},{7,6},{8,9},{9,8},{10,11... | collective-permute-start | bytes 786440 | tf_op jit(solution)/shard_map/ppermute | solution.py:287
  107.5 27.1 %collective-permute-start.35 = (bf16[2,256,512]{2,1,0:T(8,128)(2,1)S(1)}, bf16[2,256,512]{2,1,0:T(8,128)(2,1)S(1)}, u32[]{:S(2)}, u32[]{:S(2)}) collective-permute-start(bf16[2,256,512]{2,1,0:T(8,128)(2,1)S(1)} %get-tuple-element.107), channel_id=1, source_target_pairs={{0,8},{4,12},{8,0},{12,4},{16,24},{20,28},{24,16},{28,20},{1,9},{5... | collective-permute-start | bytes 1572872 | tf_op jit(solution)/shard_map/ppermute | solution.py:323
  112.9 23.0 %collective-permute-start.36 = (bf16[2,256,512]{2,1,0:T(8,128)(2,1)S(1)}, bf16[2,256,512]{2,1,0:T(8,128)(2,1)S(1)}, u32[]{:S(2)}, u32[]{:S(2)}) collective-permute-start(bf16[2,256,512]{2,1,0:T(8,128)(2,1)S(1)} %get-tuple-element.108), channel_id=1, source_target_pairs={{0,16},{4,20},{8,24},{12,28},{16,0},{20,4},{24,8},{28,12},{1,17},{... | collective-permute-start | bytes 1572872 | tf_op jit(solution)/shard_map/ppermute | solution.py:324
  114.5 19.7 %collective-permute-start.44 = (bf16[2,128,512]{2,1,0:T(8,128)(2,1)S(1)}, bf16[2,128,512]{2,1,0:T(8,128)(2,1)S(1)}, u32[]{:S(2)}, u32[]{:S(2)}) collective-permute-start(bf16[2,128,512]{2,1,0:T(8,128)(2,1)S(1)} %get-tuple-element.115), channel_id=1, source_target_pairs={{0,8},{4,12},{8,0},{12,4},{16,24},{20,28},{24,16},{28,20},{1,9},{5... | collective-permute-start | bytes 786440 | tf_op jit(solution)/shard_map/ppermute | solution.py:323
  116.1 18.4 %collective-permute-start.45 = (bf16[2,128,512]{2,1,0:T(8,128)(2,1)S(1)}, bf16[2,128,512]{2,1,0:T(8,128)(2,1)S(1)}, u32[]{:S(2)}, u32[]{:S(2)}) collective-permute-start(bf16[2,128,512]{2,1,0:T(8,128)(2,1)S(1)} %get-tuple-element.116), channel_id=1, source_target_pairs={{0,16},{4,20},{8,24},{12,28},{16,0},{20,4},{24,8},{28,12},{1,17},{... | collective-permute-start | bytes 786440 | tf_op jit(solution)/shard_map/ppermute | solution.py:324
  117.9 14.4 %collective-permute-start.24 = (bf16[136,512]{1,0:T(8,128)(2,1)S(1)}, bf16[136,512]{1,0:T(8,128)(2,1)S(1)}, u32[]{:S(2)}, u32[]{:S(2)}) collective-permute-start(bf16[136,512]{1,0:T(8,128)(2,1)S(1)} %get-tuple-element.98), channel_id=1, source_target_pairs={{0,16},{4,20},{8,24},{12,28},{16,0},{20,4},{24,8},{28,12},{1,17},{... | collective-permute-start | bytes 417800 | tf_op jit(solution)/shard_map/ppermute | solution.py:60
  132.4 16.5 %collective-permute-start.49 = (bf16[2,128,512]{2,1,0:T(8,128)(2,1)S(1)}, bf16[2,128,512]{2,1,0:T(8,128)(2,1)S(1)}, u32[]{:S(2)}, u32[]{:S(2)}) collective-permute-start(bf16[2,128,512]{2,1,0:T(8,128)(2,1)S(1)} %get-tuple-element.122), channel_id=1, source_target_pairs={{0,8},{4,12},{8,0},{12,4},{16,24},{20,28},{24,16},{28,20},{1,9},{5... | collective-permute-start | bytes 786440 | tf_op jit(solution)/shard_map/ppermute | solution.py:323
  134.3 15.2 %collective-permute-start.50 = (bf16[2,128,512]{2,1,0:T(8,128)(2,1)S(1)}, bf16[2,128,512]{2,1,0:T(8,128)(2,1)S(1)}, u32[]{:S(2)}, u32[]{:S(2)}) collective-permute-start(bf16[2,128,512]{2,1,0:T(8,128)(2,1)S(1)} %get-tuple-element.123), channel_id=1, source_target_pairs={{0,16},{4,20},{8,24},{12,28},{16,0},{20,4},{24,8},{28,12},{1,17},{... | collective-permute-start | bytes 786440 | tf_op jit(solution)/shard_map/ppermute | solution.py:324
  134.6 15.1 %collective-permute-start.26 = (bf16[136,512]{1,0:T(8,128)(2,1)S(1)}, bf16[136,512]{1,0:T(8,128)(2,1)S(1)}, u32[]{:S(2)}, u32[]{:S(2)}) collective-permute-start(bf16[136,512]{1,0:T(8,128)(2,1)S(1)} %get-tuple-element.100), channel_id=1, source_target_pairs={{0,24},{4,28},{8,16},{12,20},{16,8},{20,12},{24,0},{28,4},{1,25},{... | collective-permute-start | bytes 417800 | tf_op jit(solution)/shard_map/ppermute | solution.py:60
  135.9 15.6 %collective-permute-start.27 = (bf16[136,512]{1,0:T(8,128)(2,1)S(1)}, bf16[136,512]{1,0:T(8,128)(2,1)S(1)}, u32[]{:S(2)}, u32[]{:S(2)}) collective-permute-start(bf16[136,512]{1,0:T(8,128)(2,1)S(1)} %get-tuple-element.101), channel_id=1, source_target_pairs={{0,28},{4,24},{8,20},{12,16},{16,12},{20,8},{24,4},{28,0},{1,29},{... | collective-permute-start | bytes 417800 | tf_op jit(solution)/shard_map/ppermute | solution.py:60
  148.8 15.2 %collective-permute-start.37 = (bf16[256,512]{1,0:T(8,128)(2,1)S(1)}, bf16[256,512]{1,0:T(8,128)(2,1)S(1)}, u32[]{:S(2)}, u32[]{:S(2)}) collective-permute-start(bf16[256,512]{1,0:T(8,128)(2,1)S(1)} %get-tuple-element.111), channel_id=1, source_target_pairs={{0,16},{4,20},{8,24},{12,28},{16,0},{20,4},{24,8},{28,12},{1,17},{... | collective-permute-start | bytes 786440 | tf_op jit(solution)/shard_map/ppermute | solution.py:337
  149.4 14.6 %collective-permute-start.38 = (bf16[256,512]{1,0:T(8,128)(2,1)S(1)}, bf16[256,512]{1,0:T(8,128)(2,1)S(1)}, u32[]{:S(2)}, u32[]{:S(2)}) collective-permute-start(bf16[256,512]{1,0:T(8,128)(2,1)S(1)} %get-tuple-element.112), channel_id=1, source_target_pairs={{0,8},{4,12},{8,0},{12,4},{16,24},{20,28},{24,16},{28,20},{1,9},{5... | collective-permute-start | bytes 786440 | tf_op jit(solution)/shard_map/ppermute | solution.py:338
  (41 other events, 486.7 us)

commit v2 on v1

--- a/solution.py
+++ b/solution.py
@@ -19,18 +19,25 @@
     return pl.BlockSpec(memory_space=pltpu.VMEM)
 
 
-def call(body, outs, scratch, flops, moved, limit_mib, *args):
+def hbm():
+    return pl.BlockSpec(memory_space=pltpu.HBM)
+
+
+def call(body, outs, scratch, flops, moved, limit_mib, *args, raw=0, raw_out=False, alias=None, free=0):
     many = len(outs) > 1
-    return run_kernel(body, outs, scratch, flops, moved, limit_mib, many, *args)
-
-
-def run_kernel(body, outs, scratch, flops, moved, limit_mib, many, *args):
-    specs = [vmem()] * len(args)
+    return run_kernel(body, outs, scratch, flops, moved, limit_mib, many, args, raw, raw_out, alias, free)
+
+
+def run_kernel(body, outs, scratch, flops, moved, limit_mib, many, args, raw, raw_out, alias, free):
+    specs = [hbm()] * raw + [pl.BlockSpec(memory_space=pl.ANY)] * free
+    specs += [vmem()] * (len(args) - raw - free)
+    out_spec = hbm() if raw_out else vmem()
     got = pl.pallas_call(
         body,
         out_shape=tuple(outs) if many else outs[0],
         in_specs=specs,
-        out_specs=tuple([vmem()] * len(outs)) if many else vmem(),
+        out_specs=tuple([out_spec] * len(outs)) if many else out_spec,
+        input_output_aliases=alias or {},
         scratch_shapes=scratch,
         cost_estimate=pl.CostEstimate(
             flops=int(flops), bytes_accessed=int(moved), transcendentals=0
@@ -61,14 +68,51 @@
     return got
 
 
-def mixed_body(count, piece, group, key, value, taps, *outs):
+def mixed_body(count, piece, group, key, value, taps, *refs):
+    outs = refs[:count]
+    key_in, value_in, taps_in, block_out, sems = refs[-5:]
     me = lax.axis_index("seq")
-    for k in range(count):
-        dest = me ^ k
-        rows = pl.ds(pl.multiple_of(dest * piece, piece), piece)
-        outs[k][0:piece, :] = (key[rows, :].astype(F32) * value[rows, :].astype(F32)).astype(BF16)
-        row = taps[pl.ds(dest * piece // group, 1), :]
-        outs[k][piece : piece + EXTRA, :] = jnp.broadcast_to(row, (EXTRA, row.shape[1])).astype(BF16)
+    row_copy = pltpu.make_async_copy(taps, taps_in, sems.at[3 * count])
+    row_copy.start()
+    copies = []
+    for k in range(count):
+        rows = pl.ds(pl.multiple_of((me ^ k) * piece, piece), piece)
+        pair = (
+            pltpu.make_async_copy(key.at[rows, :], key_in.at[k], sems.at[3 * k]),
+            pltpu.make_async_copy(value.at[rows, :], value_in.at[k], sems.at[3 * k + 1]),
+        )
+        for copy in pair:
+            copy.start()
+        copies.append(pair)
+    row_copy.wait()
+    for k in range(count):
+        for copy in copies[k]:
+            copy.wait()
+        block_out[k, 0:piece, :] = (key_in[k].astype(F32) * value_in[k].astype(F32)).astype(BF16)
+        row = taps_in[pl.ds((me ^ k) * piece // group, 1), :]
+        block_out[k, piece : piece + EXTRA, :] = jnp.broadcast_to(row, (EXTRA, row.shape[1])).astype(BF16)
+        pltpu.make_async_copy(block_out.at[k], outs[k], sems.at[3 * k + 2]).start()
+    for k in range(count):
+        pltpu.make_async_copy(block_out.at[k], outs[k], sems.at[3 * k + 2]).wait()
+
+
+def mixed_keep_body(count, piece, group, key, value, taps, block, *refs):
+    outs, keeps = refs[:count], refs[count : count + 2]
+    keep_in, keep_sems = refs[-2:]
+    rows = keep_in.shape[1]
+    first = (lax.axis_index("seq") & 1) * block.shape[0] // 2
+    for n in range(QUARTERS):
+        here = pl.ds(pl.multiple_of(first + n * rows, rows), rows)
+        pltpu.make_async_copy(block.at[here, :], keep_in.at[n], keep_sems.at[2 * n]).start()
+    mixed_body(count, piece, group, key, value, taps, *outs, *refs[count + 2 : -2])
+    for n in range(QUARTERS):
+        here = pl.ds(pl.multiple_of(first + n * rows, rows), rows)
+        pltpu.make_async_copy(block.at[here, :], keep_in.at[n], keep_sems.at[2 * n]).wait()
+        to = keeps[n // 2].at[n % 2, 0]
+        pltpu.make_async_copy(keep_in.at[n], to, keep_sems.at[2 * n + 1]).start()
+    for n in range(QUARTERS):
+        to = keeps[n // 2].at[n % 2, 0]
+        pltpu.make_async_copy(keep_in.at[n], to, keep_sems.at[2 * n + 1]).wait()
 
 
 def upstream_body(count, piece, grad, query, *outs):
@@ -155,13 +199,15 @@
 def query_body(count, piece, *refs):
     me = lax.axis_index("seq")
     slots = refs[:count]
-    query, grad, mixed, grad_query = refs[count:]
+    query, grad, mixed, grad_query, again = refs[count:]
     for k in range(count):
         pos = me ^ k
         rows = pl.ds(pl.multiple_of(pos * piece, piece), piece)
         conv = slots[k][...].astype(F32)
         mixed[rows, :] = (query[rows, :].astype(F32) * conv).astype(BF16)
-        grad_query[rows, :] = (grad[rows, :].astype(F32) * conv).astype(BF16)
+        value = (grad[rows, :].astype(F32) * conv).astype(BF16)
+        grad_query[rows, :] = value
+        again[rows, :] = value
 
 
 def key_body(count, piece, group, factor, *refs):
@@ -182,14 +228,20 @@
     taps_grad[...] = total * factor
 
 
-def stack_body(block, other, *outs):
+def stack_body(kept_x, kept_y, other, *refs):
+    del kept_x, kept_y
+    outs, sems = refs[:-1], refs[-1]
     rows = outs[0].shape[2]
-    first = (lax.axis_index("seq") & 1) * block.shape[0] // 2
+    first = (lax.axis_index("seq") & 1) * other.shape[0] // 2
+    copies = []
     for n in range(QUARTERS):
         here = pl.ds(pl.multiple_of(first + n * rows, rows), rows)
-        out = outs[n // 2]
-        out[n % 2, 0] = block[here, :]
-        out[n % 2, 1] = other[here, :]
+        to = outs[n // 2].at[n % 2, 1]
+        copies.append(pltpu.make_async_copy(other.at[here, :], to, sems.at[n]))
+    for copy in copies:
+        copy.start()
+    for copy in copies:
+        copy.wait()
 
 
 def weight_body(chans, start, last, own_grad, other_grad, *refs):
@@ -237,8 +289,8 @@
     out_q[...] = (keep_q[...] + got_q[1].astype(F32)).astype(BF16)
 
 
-def finish_body(chunks, factor, *refs):
-    out = refs[-1]
+def finish_body(chunks, begin, factor, *refs):
+    out, block, sem = refs[-3:]
     half = refs[0].shape[1] // 2
     first = 0
     for n in range(chunks):
@@ -247,8 +299,16 @@
         first += mine.shape[0]
         left = mine[:, :half] + got_p[0].astype(F32) + last_p[...].astype(F32)
         right = mine[:, half:] + got_q[0].astype(F32) + last_q[...].astype(F32)
-        out[here, :half] = left * factor
-        out[here, half:] = right * factor
+        block[here, :half] = left * factor
+        block[here, half:] = right * factor
+    copy = pltpu.make_async_copy(block, out.at[pl.ds(begin, first), :], sem)
+    copy.start()
+    copy.wait()
+
+
+def last_body(chunks, begin, factor, whole, *refs):
+    del whole
+    finish_body(chunks, begin, factor, *refs)
 
 
 def plane_pairs(seqs, chans):
@@ -261,16 +321,13 @@
     return outer, middle
 
 
-def weight_start(layer_input):
-    channels, tok = layer_input.shape
+def weight_start(other, kept):
     seqs, chans = lax.axis_size("seq"), lax.axis_size("chan")
-    half = channels // 2
-    swap = [(i, i ^ 1) for i in range(seqs)]
-    other = lax.ppermute(layer_input, "seq", swap)
-    quarter = struct((QUARTERS // 2, 2, half // QUARTERS, tok), BF16)
+    quarter = struct(kept[0].shape, BF16)
     own = call(
-        stack_body, [quarter] * 2, [], half * tok, 4 * half * tok, 58,
-        layer_input, other,
+        stack_body, [quarter] * 2, [pltpu.SemaphoreType.DMA((QUARTERS,))],
+        other.size, 2 * other.size, 8,
+        *kept, other, raw=2, free=1, raw_out=True, alias={0: 0, 1: 1},
     )
     outer, middle = plane_pairs(seqs, chans)
     both = ("seq", "chan")
@@ -315,7 +372,7 @@
             [pltpu.VMEM((2, chans * rows, tok), BF16)],
             4 * chans * rows * outputs * tok,
             12 << 20,
-            20,
+            12,
             grad_query,
             other_grad,
             *sources,
@@ -337,14 +394,20 @@
         last_p = lax.ppermute(next_p, "seq", across)
         last_q = lax.ppermute(next_q, "seq", along)
         parts += [mine, got_p, got_q, last_p, last_q]
+    total = QUARTERS * gathered[0][3][0].shape[2]
+    result = struct((total, outputs), F32)
+    early = total - parts[-5].shape[0]
     (out,) = call(
-        functools.partial(finish_body, len(gathered), factor),
-        [struct((QUARTERS * gathered[0][3][0].shape[2], outputs), F32)],
-        [],
-        3 * outputs * outputs,
-        8 << 20,
-        16,
-        *parts,
+        functools.partial(finish_body, len(gathered) - 1, 0, factor),
+        [result], [pltpu.VMEM((early, outputs), F32), pltpu.SemaphoreType.DMA],
+        3 * early * outputs, 8 * early * outputs, 12,
+        *parts[:-5], raw_out=True,
+    )
+    (out,) = call(
+        functools.partial(last_body, 1, early, factor),
+        [result], [pltpu.VMEM((total - early, outputs), F32), pltpu.SemaphoreType.DMA],
+        3 * outputs * (total - early), 8 * outputs * (total - early), 8,
+        out, *parts[-5:], raw=1, raw_out=True, alias={0: 0},
     )
     return out
 
@@ -379,11 +442,31 @@
     unit = channels * tok
     work = unit * tok * (seqs + 1)
 
-    mixed = call(
-        functools.partial(mixed_body, seqs, piece, group),
-        [large] * seqs, [], 3 * unit, 6 * unit, 58,
-        key_proj, value_proj, filter_taps,
-    )
+    buffers = [
+        pltpu.VMEM((seqs, piece, tok), BF16),
+        pltpu.VMEM((seqs, piece, tok), BF16),
+        pltpu.VMEM(filter_taps.shape, F32),
+        pltpu.VMEM((seqs, piece + EXTRA, tok), BF16),
+        pltpu.SemaphoreType.DMA((3 * seqs + 1,)),
+    ]
+    first_args = (key_proj, value_proj, filter_taps)
+    if special:
+        other = lax.ppermute(layer_input, "seq", [(i, i ^ 1) for i in range(seqs)])
+        rows = channels // 2 // QUARTERS
+        first = call(
+            functools.partial(mixed_keep_body, seqs, piece, group),
+            [large] * seqs + [struct((QUARTERS // 2, 2, rows, tok), BF16)] * 2,
+            buffers + [pltpu.VMEM((QUARTERS, rows, tok), BF16), pltpu.SemaphoreType.DMA((2 * QUARTERS,))],
+            3 * unit, 8 * unit, 58,
+            *first_args, layer_input, raw=4, raw_out=True,
+        )
+        mixed, kept = first[:seqs], first[seqs:]
+    else:
+        mixed = call(
+            functools.partial(mixed_body, seqs, piece, group),
+            [large] * seqs, buffers, 3 * unit, 6 * unit, 58,
+            *first_args, raw=3, raw_out=True,
+        )
     mixed_slots = exchange_slots(mixed, "seq")
     upstream = call(
         functools.partial(upstream_body, seqs, piece),
@@ -392,25 +475,25 @@
     )
     up_slots = exchange_slots(upstream, "seq")
     if special:
-        gathered = weight_start(layer_input)
+        gathered = weight_start(other, kept)
     conv = call(
         functools.partial(conv_body, seqs, piece),
         [small] * seqs + [struct((seqs, tok, tok), BF16)],
         [flat, rows8, wide, square],
-        work, 16 * unit, 22,
+        work, 16 * unit, 14,
         *mixed_slots,
     )
     conv_slots = exchange_slots(conv[:seqs], "seq")
-    mixed_out, grad_query = call(
+    mixed_out, grad_query, own_grad = call(
         functools.partial(query_body, seqs, piece),
-        [struct((channels, tok), BF16)] * 2, [], 4 * unit, 10 * unit, 16,
+        [struct((channels, tok), BF16)] * 3, [], 4 * unit, 10 * unit, 16,
         *conv_slots, query_proj, grad_out,
     )
     back = call(
         functools.partial(back_body, seqs, piece),
         [large] * seqs,
         [flat, flat, wide, square, rows8],
-        2 * work, 20 * unit, 24,
+        2 * work, 20 * unit, 18,
         *up_slots, *mixed_slots, conv[seqs],
     )
     back_slots = exchange_slots(back, "seq")
@@ -421,7 +504,7 @@
         *back_slots, key_proj, value_proj,
     )
     if special:
-        weight_grad = weight_finish(gathered, grad_query, weight_factor)
+        weight_grad = weight_finish(gathered, own_grad, weight_factor)
     else:
         weight_grad = weight_general(layer_input, grad_query, weight_factor)
     return (mixed_out, grad_query, grad_key, grad_value, filter_grad, weight_grad)

time: 166 us -> 157 us (0.946)
  starting transfers between devices: 82.8 us -> 71.5 us
  waiting for transfers between devices: 50.7 us -> 54.5 us
  local copies, waits for them, and re-layouts: 4.38 us -> 1.89 us
    ppermute x1, starting transfers between devices: 11.2 us -> 0.92 us  [weight_start(): a3x = lax.ppermute(b2x, 'chan', outer)]
    ppermute x1, starting transfers between devices: 13.3 us -> 4.24 us  [weight_start(): a2x = lax.ppermute(b1x, 'chan', outer)]
    ppermute x3, waiting for transfers between devices: 8.86 us -> 0.26 us  [weight_finish(): last_q = lax.ppermute(next_q, 'seq', along)]
    ppermute x3, waiting for transfers between devices: 0.01 us -> 7.05 us  [weight_finish(): got_p = lax.ppermute(send_p, 'seq', along)]
    ppermute x28, waiting for transfers between devices: 37.6 us -> 31.2 us  [exchange_slots(): got.append(lax.ppermute(pieces[k], axis, pairs))]
    ppermute x1, starting transfers between devices: 10.2 us -> 15.9 us  [weight_start(): a2y = lax.ppermute(b1y, 'chan', outer)]
    ppermute x3, waiting for transfers between devices: 0.22 us -> 5.6 us  [weight_finish(): last_p = lax.ppermute(next_p, 'seq', across)]
    ppermute x1, waiting for transfers between devices: 0.01 us -> 2.56 us  [weight_start(): a2y = lax.ppermute(b1y, 'chan', outer)]
  transfers between devices with their start and end apart: 53 -> 53, of which waited for: 14 -> 17; matrix products, arithmetic and copies ran while one was open for 0% -> 0% of each run, Pallas kernels for 15% -> 17%
where the time goes in v2:
time: 157 us; the launch traced here: 156 us
  starting transfers between devices  71.5 us (46%)
  waiting for transfers between devices  54.5 us (35%)
  Pallas kernels  27.5 us (18%)
  local copies, waits for them, and re-layouts  1.89 us (1%)
    ppermute x28, waiting for transfers between devices, exchange_slots(): got.append(lax.ppermute(pieces[k], axis, pairs))  31.2 us
    ppermute x28, starting transfers between devices, exchange_slots(): got.append(lax.ppermute(pieces[k], axis, pairs))  30.3 us
    pallas_call x15, Pallas kernels, run_kernel(): pl.pallas_call(body, out_shape=tuple(outs) if many else outs[0], in_specs...  27.5 us
    ppermute x1, starting transfers between devices, weight_start(): a2y = lax.ppermute(b1y, 'chan', outer)  15.9 us
    ppermute x3, waiting for transfers between devices, weight_finish(): got_p = lax.ppermute(send_p, 'seq', along)  7.05 us
    ppermute x1, waiting for transfers between devices, weight_start(): a3y = lax.ppermute(b2y[0:1], 'chan', outer)  5.61 us
    ppermute x3, waiting for transfers between devices, weight_finish(): last_p = lax.ppermute(next_p, 'seq', across)  5.6 us
    ppermute x3, starting transfers between devices, weight_finish(): last_q = lax.ppermute(next_q, 'seq', along)  4.69 us
  transfers between devices with their start and end apart: 53, of which 17 were waited for; matrix products, arithmetic and copies ran while one was open for 0% of the time, Pallas kernels for 17%

profile of v2, /device:TPU:0, one launch (start us, length us, event | category | flops | bytes accessed | tf_op | source)
XLA Modules:
  0.0 156.4 jit_solution(18306237430953451786)
XLA Ops:
  1.2 3.6 %shard_map.109 = (bf16[136,512]{1,0:T(8,128)(2,1)}, bf16[136,512]{1,0:T(8,128)(2,1)}, bf16[136,512]{1,0:T(8,128)(2,1)}, bf16[136,512]{1,0:T(8,128)(2,1)}, bf16[1...) custom-call(bf16[1024,512]{1,0:T(8,128)(2,1)} %refs_8_.3, ...), custom_call_target="tpu_custom_call" | custom-call | flops 1572864 | bytes 4194304 | tf_op jit(solution)/shard_map/pallas_call | solution.py:35
  4.9 2.8 %collective-permute-start.1 = (bf16[136,512]{1,0:T(8,128)(2,1)}, bf16[136,512]{1,0:T(8,128)(2,1)S(1)}, u32[]{:S(2)}, u32[]{:S(2)}) collective-permute-start(bf16[136,512]{1,0:T(8,128)(2,1)} %get-tuple-element.72), channel_id=1, source_target_pairs={{0,8},{4,12},{8,0},{12,4},{16,24},{20,28},{24,16},{28,20},{1,9},{5... | collective-permute-start | bytes 417800 | tf_op jit(solution)/shard_map/ppermute | solution.py:67
  9.6 3.0 %collective-permute-done.1.refs_2_.refs_10_ = bf16[136,512]{1,0:T(8,128)(2,1)S(1)} collective-permute-done((bf16[136,512]{1,0:T(8,128)(2,1)}, bf16[136,512]{1,0:T(8,128)(2,1)S(1)}, u32[]{:S(2)}, u32[]{:S(2)}) %collective-permute-start.1) | collective-permute-done | bytes 139296 | tf_op jit(solution)/shard_map/ppermute | solution.py:67
  12.5 3.0 %collective-permute-start.5 = (bf16[136,512]{1,0:T(8,128)(2,1)}, bf16[136,512]{1,0:T(8,128)(2,1)S(1)}, u32[]{:S(2)}, u32[]{:S(2)}) collective-permute-start(bf16[136,512]{1,0:T(8,128)(2,1)} %get-tuple-element.76), channel_id=1, source_target_pairs={{0,24},{4,28},{8,16},{12,20},{16,8},{20,12},{24,0},{28,4},{1,25},{... | collective-permute-start | bytes 417800 | tf_op jit(solution)/shard_map/ppermute | solution.py:67
  24.4 4.0 %shard_map.110 = (bf16[128,512]{1,0:T(8,128)(2,1)S(1)}, bf16[128,512]{1,0:T(8,128)(2,1)S(1)}, bf16[128,512]{1,0:T(8,128)(2,1)S(1)}, bf16[128,512]{1,0:T(8,128)(2...) custom-call(bf16[136,512]{1,0:T(8,128)(2,1)S(1)} %copy-done.7, ...), custom_call_target="tpu_custom_call" | custom-call | flops 2415919104 | bytes 8388608 | tf_op jit(solution)/shard_map/pallas_call | solution.py:35
  32.7 2.2 %collective-permute-done.8.refs_2_ = bf16[128,512]{1,0:T(8,128)(2,1)S(1)} collective-permute-done((bf16[128,512]{1,0:T(8,128)(2,1)S(1)}, bf16[128,512]{1,0:T(8,128)(2,1)S(1)}, u32[]{:S(2)}, u32[]{:S(2)}) %collective-permute-start.8) | collective-permute-done | bytes 131104 | tf_op jit(solution)/shard_map/ppermute | solution.py:67
  35.0 2.9 %collective-permute-start.12 = (bf16[128,512]{1,0:T(8,128)(2,1)S(1)}, bf16[128,512]{1,0:T(8,128)(2,1)S(1)}, u32[]{:S(2)}, u32[]{:S(2)}) collective-permute-start(bf16[128,512]{1,0:T(8,128)(2,1)S(1)} %get-tuple-element.84), channel_id=1, source_target_pairs={{0,24},{4,28},{8,16},{12,20},{16,8},{20,12},{24,0},{28,4},{1,25},{... | collective-permute-start | bytes 393224 | tf_op jit(solution)/shard_map/ppermute | solution.py:67
  37.9 2.5 %collective-permute-start.13 = (bf16[128,512]{1,0:T(8,128)(2,1)S(1)}, bf16[128,512]{1,0:T(8,128)(2,1)S(1)}, u32[]{:S(2)}, u32[]{:S(2)}) collective-permute-start(bf16[128,512]{1,0:T(8,128)(2,1)S(1)} %get-tuple-element.85), channel_id=1, source_target_pairs={{0,28},{4,24},{8,20},{12,16},{16,12},{20,8},{24,4},{28,0},{1,29},{... | collective-permute-start | bytes 393224 | tf_op jit(solution)/shard_map/ppermute | solution.py:67
  42.0 2.7 %collective-permute-done.11.refs_5_ = bf16[128,512]{1,0:T(8,128)(2,1)S(1)} collective-permute-done((bf16[128,512]{1,0:T(8,128)(2,1)S(1)}, bf16[128,512]{1,0:T(8,128)(2,1)S(1)}, u32[]{:S(2)}, u32[]{:S(2)}) %collective-permute-start.11) | collective-permute-done | bytes 131104 | tf_op jit(solution)/shard_map/ppermute | solution.py:67
  49.0 2.8 %collective-permute-done.17.refs_4_ = bf16[128,512]{1,0:T(8,128)(2,1)S(1)} collective-permute-done((bf16[128,512]{1,0:T(8,128)(2,1)S(1)}, bf16[128,512]{1,0:T(8,128)(2,1)S(1)}, u32[]{:S(2)}, u32[]{:S(2)}) %collective-permute-start.17) | collective-permute-done | bytes 131104 | tf_op jit(solution)/shard_map/ppermute | solution.py:67
  53.5 2.4 %collective-permute-start.19 = (bf16[128,512]{1,0:T(8,128)(2,1)S(1)}, bf16[128,512]{1,0:T(8,128)(2,1)S(1)}, u32[]{:S(2)}, u32[]{:S(2)}) collective-permute-start(bf16[128,512]{1,0:T(8,128)(2,1)S(1)} %get-tuple-element.94), channel_id=1, source_target_pairs={{0,24},{4,28},{8,16},{12,20},{16,8},{20,12},{24,0},{28,4},{1,25},{... | collective-permute-start | bytes 393224 | tf_op jit(solution)/shard_map/ppermute | solution.py:67
  55.9 4.3 %collective-permute-done.19.refs_6_ = bf16[128,512]{1,0:T(8,128)(2,1)S(1)} collective-permute-done((bf16[128,512]{1,0:T(8,128)(2,1)S(1)}, bf16[128,512]{1,0:T(8,128)(2,1)S(1)}, u32[]{:S(2)}, u32[]{:S(2)}) %collective-permute-start.19) | collective-permute-done | bytes 131104 | tf_op jit(solution)/shard_map/ppermute | solution.py:67
  61.7 5.2 %collective-permute-done.20.refs_7_ = bf16[128,512]{1,0:T(8,128)(2,1)S(1)} collective-permute-done((bf16[128,512]{1,0:T(8,128)(2,1)S(1)}, bf16[128,512]{1,0:T(8,128)(2,1)S(1)}, u32[]{:S(2)}, u32[]{:S(2)}) %collective-permute-start.20) | collective-permute-done | bytes 131104 | tf_op jit(solution)/shard_map/ppermute | solution.py:67
  67.4 4.2 %collective-permute-start.32 = (bf16[2,2,128,512]{3,2,1,0:T(8,128)(2,1)S(1)}, bf16[2,2,128,512]{3,2,1,0:T(8,128)(2,1)S(1)}, u32[]{:S(2)}, u32[]{:S(2)}) collective-permute-start(bf16[2,2,128,512]{3,2,1,0:T(8,128)(2,1)S(1)} %collective-permute-done.31.refs_4_), channel_id=1, source_target_pairs={{0,1},{1,0},{2,3},{3,2},{4,5},{5,4},{6,7},{7,6},{8,9},{9,8},{10,11... | collective-permute-start | bytes 1572872 | tf_op jit(solution)/shard_map/ppermute | solution.py:338
  72.5 6.4 %shard_map.113 = (bf16[136,512]{1,0:T(8,128)(2,1)S(1)}, bf16[136,512]{1,0:T(8,128)(2,1)S(1)}, bf16[136,512]{1,0:T(8,128)(2,1)S(1)}, bf16[136,512]{1,0:T(8,128)(2...) custom-call(bf16[128,512]{1,0:T(8,128)(2,1)S(1)} %get-tuple-element., ...), custom_call_target="tpu_custom_call" | custom-call | flops 4831838208 | bytes 10485760 | tf_op jit(solution)/shard_map/pallas_call | solution.py:35
  79.0 15.9 %collective-permute-start.41 = (bf16[2,2,128,512]{3,2,1,0:T(8,128)(2,1)S(1)}, bf16[2,2,128,512]{3,2,1,0:T(8,128)(2,1)S(1)}, u32[]{:S(2)}, u32[]{:S(2)}) collective-permute-start(bf16[2,2,128,512]{3,2,1,0:T(8,128)(2,1)S(1)} %collective-permute-done.40.refs_4_), channel_id=1, source_target_pairs={{0,1},{1,0},{2,3},{3,2},{4,5},{5,4},{6,7},{7,6},{8,9},{9,8},{10,11... | collective-permute-start | bytes 1572872 | tf_op jit(solution)/shard_map/ppermute | solution.py:341
  97.8 3.8 %shard_map.116 = (f32[256,1024]{1,0:T(8,128)S(1)}, bf16[2,256,512]{2,1,0:T(8,128)(2,1)S(1)}, bf16[2,256,512]{2,1,0:T(8,128)(2,1)S(1)}, f32[256,512]{1,0:T(8,128)S(1)}, f32[256,512]{1,0:T(8,128)S(1)}) custom-call(bf16[1024,512]{1,0:T(8,128)(2,1)S(1)} %get-tuple-element.108.own_grad, bf16[1024,512]{1,0:T(8,128)(2,1)S(1)} %collective-permute-done.28.other_grad, ...), custom_call_target="tpu_custom_call" | custom-call | flops 2147483648 | bytes 12582912 | tf_op jit(solution)/shard_map/pallas_call | solution.py:35
  105.1 2.6 %collective-permute-done.41.refs_2_ = bf16[2,2,128,512]{3,2,1,0:T(8,128)(2,1)S(1)} collective-permute-done((bf16[2,2,128,512]{3,2,1,0:T(8,128)(2,1)S(1)}, bf16[2,2,128,512]{3,2,1,0:T(8,128)(2,1)S(1)}, u32[]{:S(2)}, u32[]{:S(2)}) %collective-permute-start.41) | collective-permute-done | bytes 524320 | tf_op jit(solution)/shard_map/ppermute | solution.py:341
  107.7 5.6 %collective-permute-done.43.refs_3_ = bf16[1,2,128,512]{3,2,1,0:T(8,128)(2,1)S(1)} collective-permute-done((bf16[1,2,128,512]{3,2,1,0:T(8,128)(2,1)S(1)}, bf16[1,2,128,512]{3,2,1,0:T(8,128)(2,1)S(1)}, u32[]{:S(2)}, u32[]{:S(2)}) %collective-permute-start.43) | collective-permute-done | bytes 262176 | tf_op jit(solution)/shard_map/ppermute | solution.py:343
  113.3 2.2 %collective-permute-start.26 = (bf16[136,512]{1,0:T(8,128)(2,1)S(1)}, bf16[136,512]{1,0:T(8,128)(2,1)S(1)}, u32[]{:S(2)}, u32[]{:S(2)}) collective-permute-start(bf16[136,512]{1,0:T(8,128)(2,1)S(1)} %get-tuple-element.103), channel_id=1, source_target_pairs={{0,24},{4,28},{8,16},{12,20},{16,8},{20,12},{24,0},{28,4},{1,25},{... | collective-permute-start | bytes 417800 | tf_op jit(solution)/shard_map/ppermute | solution.py:67
  116.9 6.8 %collective-permute-done.25.refs_5_ = bf16[136,512]{1,0:T(8,128)(2,1)S(1)} collective-permute-done((bf16[136,512]{1,0:T(8,128)(2,1)S(1)}, bf16[136,512]{1,0:T(8,128)(2,1)S(1)}, u32[]{:S(2)}, u32[]{:S(2)}) %collective-permute-start.25) | collective-permute-done | bytes 139296 | tf_op jit(solution)/shard_map/ppermute | solution.py:67
  129.3 3.5 %collective-permute-done.44.got_p.refs_6_ = bf16[2,128,512]{2,1,0:T(8,128)(2,1)S(1)} collective-permute-done((bf16[2,128,512]{2,1,0:T(8,128)(2,1)S(1)}, bf16[2,128,512]{2,1,0:T(8,128)(2,1)S(1)}, u32[]{:S(2)}, u32[]{:S(2)}) %collective-permute-start.44) | collective-permute-done | bytes 262176 | tf_op jit(solution)/shard_map/ppermute | solution.py:380
  134.9 3.5 %collective-permute-done.49.got_p.refs_1_ = bf16[2,128,512]{2,1,0:T(8,128)(2,1)S(1)} collective-permute-done((bf16[2,128,512]{2,1,0:T(8,128)(2,1)S(1)}, bf16[2,128,512]{2,1,0:T(8,128)(2,1)S(1)}, u32[]{:S(2)}, u32[]{:S(2)}) %collective-permute-start.49) | collective-permute-done | bytes 262176 | tf_op jit(solution)/shard_map/ppermute | solution.py:380
  144.6 5.6 %collective-permute-done.46.refs_8_ = bf16[128,512]{1,0:T(8,128)(2,1)S(1)} collective-permute-done((bf16[128,512]{1,0:T(8,128)(2,1)S(1)}, bf16[128,512]{1,0:T(8,128)(2,1)S(1)}, u32[]{:S(2)}, u32[]{:S(2)}) %collective-permute-start.46) | collective-permute-done | bytes 131104 | tf_op jit(solution)/shard_map/ppermute | solution.py:394
  (114 shorter events, 54.0 us)
Async XLA Ops:
  0.7 14.8 %collective-permute-start.29 = (bf16[1024,512]{1,0:T(8,128)(2,1)}, bf16[1024,512]{1,0:T(8,128)(2,1)S(1)}, u32[]{:S(2)}, u32[]{:S(2)}) collective-permute-start(bf16[1024,512]{1,0:T(8,128)(2,1)} %block.1), channel_id=1, source_target_pairs={{0,4},{4,0},{8,12},{12,8},{16,20},{20,16},{24,28},{28,24},{1,5},{5... | collective-permute-start | bytes 3145736 | tf_op jit(solution)/shard_map/ppermute | solution.py:454
  7.8 12.1 %collective-permute-start.3 = (bf16[136,512]{1,0:T(8,128)(2,1)}, bf16[136,512]{1,0:T(8,128)(2,1)S(1)}, u32[]{:S(2)}, u32[]{:S(2)}) collective-permute-start(bf16[136,512]{1,0:T(8,128)(2,1)} %get-tuple-element.74), channel_id=1, source_target_pairs={{0,16},{4,20},{8,24},{12,28},{16,0},{20,4},{24,8},{28,12},{1,17},{... | collective-permute-start | bytes 417800 | tf_op jit(solution)/shard_map/ppermute | solution.py:67
  9.3 13.1 %collective-permute-start.4 = (bf16[136,512]{1,0:T(8,128)(2,1)}, bf16[136,512]{1,0:T(8,128)(2,1)S(1)}, u32[]{:S(2)}, u32[]{:S(2)}) collective-permute-start(bf16[136,512]{1,0:T(8,128)(2,1)} %get-tuple-element.75), channel_id=1, source_target_pairs={{0,20},{4,16},{8,28},{12,24},{16,4},{20,0},{24,12},{28,8},{1,21},{... | collective-permute-start | bytes 417800 | tf_op jit(solution)/shard_map/ppermute | solution.py:67
  18.1 27.3 %collective-permute-start.30 = (bf16[2,2,128,512]{3,2,1,0:T(8,128)(2,1)}, bf16[2,2,128,512]{3,2,1,0:T(8,128)(2,1)S(1)}, u32[]{:S(2)}, u32[]{:S(2)}) collective-permute-start(bf16[2,2,128,512]{3,2,1,0:T(8,128)(2,1)} %get-tuple-element.111.refs_0_), channel_id=1, source_target_pairs={{0,1},{1,0},{2,3},{3,2},{4,5},{5,4},{6,7},{7,6},{8,9},{9,8},{10,11... | collective-permute-start | bytes 1572872 | tf_op jit(solution)/shard_map/ppermute | solution.py:334
  32.5 12.2 %collective-permute-start.11 = (bf16[128,512]{1,0:T(8,128)(2,1)S(1)}, bf16[128,512]{1,0:T(8,128)(2,1)S(1)}, u32[]{:S(2)}, u32[]{:S(2)}) collective-permute-start(bf16[128,512]{1,0:T(8,128)(2,1)S(1)} %get-tuple-element.83), channel_id=1, source_target_pairs={{0,20},{4,16},{8,28},{12,24},{16,4},{20,0},{24,12},{28,8},{1,21},{... | collective-permute-start | bytes 393224 | tf_op jit(solution)/shard_map/ppermute | solution.py:67
  40.4 26.5 %collective-permute-start.39 = (bf16[2,2,128,512]{3,2,1,0:T(8,128)(2,1)S(1)}, bf16[2,2,128,512]{3,2,1,0:T(8,128)(2,1)S(1)}, u32[]{:S(2)}, u32[]{:S(2)}) collective-permute-start(bf16[2,2,128,512]{3,2,1,0:T(8,128)(2,1)S(1)} %copy-done.2), channel_id=1, source_target_pairs={{0,1},{1,0},{2,3},{3,2},{4,5},{5,4},{6,7},{7,6},{8,9},{9,8},{10,11... | collective-permute-start | bytes 1572872 | tf_op jit(solution)/shard_map/ppermute | solution.py:336
  44.7 22.7 %collective-permute-start.31 = (bf16[2,2,128,512]{3,2,1,0:T(8,128)(2,1)}, bf16[2,2,128,512]{3,2,1,0:T(8,128)(2,1)S(1)}, u32[]{:S(2)}, u32[]{:S(2)}) collective-permute-start(bf16[2,2,128,512]{3,2,1,0:T(8,128)(2,1)} %get-tuple-element.111.refs_0_), channel_id=1, source_target_pairs={{0,4},{1,2},{2,1},{3,7},{4,0},{5,6},{6,5},{7,3},{8,12},{9,10},{10,... | collective-permute-start | bytes 1572872 | tf_op jit(solution)/shard_map/ppermute | solution.py:335
  45.3 26.3 %collective-permute-start.33 = (bf16[2,2,128,512]{3,2,1,0:T(8,128)(2,1)S(1)}, bf16[2,2,128,512]{3,2,1,0:T(8,128)(2,1)S(1)}, u32[]{:S(2)}, u32[]{:S(2)}) collective-permute-start(bf16[2,2,128,512]{3,2,1,0:T(8,128)(2,1)S(1)} %collective-permute-done.30.refs_1_), channel_id=1, source_target_pairs={{0,4},{1,2},{2,1},{3,7},{4,0},{5,6},{6,5},{7,3},{8,12},{9,10},{10,... | collective-permute-start | bytes 1572872 | tf_op jit(solution)/shard_map/ppermute | solution.py:339
  51.8 44.7 %collective-permute-start.28 = (bf16[1024,512]{1,0:T(8,128)(2,1)S(1)}, bf16[1024,512]{1,0:T(8,128)(2,1)S(1)}, u32[]{:S(2)}, u32[]{:S(2)}) collective-permute-start(bf16[1024,512]{1,0:T(8,128)(2,1)S(1)} %get-tuple-element.108.own_grad), channel_id=1, source_target_pairs={{0,4},{4,0},{8,12},{12,8},{16,20},{20,16},{24,28},{28,24},{1,5},{5... | collective-permute-start | bytes 3145736 | tf_op jit(solution)/shard_map/ppermute | solution.py:359
  67.4 29.1 %collective-permute-start.32 = (bf16[2,2,128,512]{3,2,1,0:T(8,128)(2,1)S(1)}, bf16[2,2,128,512]{3,2,1,0:T(8,128)(2,1)S(1)}, u32[]{:S(2)}, u32[]{:S(2)}) collective-permute-start(bf16[2,2,128,512]{3,2,1,0:T(8,128)(2,1)S(1)} %collective-permute-done.31.refs_4_), channel_id=1, source_target_pairs={{0,1},{1,0},{2,3},{3,2},{4,5},{5,4},{6,7},{7,6},{8,9},{9,8},{10,11... | collective-permute-start | bytes 1572872 | tf_op jit(solution)/shard_map/ppermute | solution.py:338
  71.6 26.2 %collective-permute-start.34 = (bf16[2,2,128,512]{3,2,1,0:T(8,128)(2,1)S(1)}, bf16[2,2,128,512]{3,2,1,0:T(8,128)(2,1)S(1)}, u32[]{:S(2)}, u32[]{:S(2)}) collective-permute-start(bf16[2,2,128,512]{3,2,1,0:T(8,128)(2,1)S(1)} %collective-permute-done.33.refs_5_), channel_id=1, source_target_pairs={{0,1},{1,0},{2,3},{3,2},{4,5},{5,4},{6,7},{7,6},{8,9},{9,8},{10,11... | collective-permute-start | bytes 1572872 | tf_op jit(solution)/shard_map/ppermute | solution.py:340
  78.9 16.0 %collective-permute-start.21 = (bf16[136,512]{1,0:T(8,128)(2,1)S(1)}, bf16[136,512]{1,0:T(8,128)(2,1)S(1)}, u32[]{:S(2)}, u32[]{:S(2)}) collective-permute-start(bf16[136,512]{1,0:T(8,128)(2,1)S(1)} %get-tuple-element.98), channel_id=1, source_target_pairs={{0,4},{4,0},{8,12},{12,8},{16,20},{20,16},{24,28},{28,24},{1,5},{5... | collective-permute-start | bytes 417800 | tf_op jit(solution)/shard_map/ppermute | solution.py:67
  79.0 28.7 %collective-permute-start.41 = (bf16[2,2,128,512]{3,2,1,0:T(8,128)(2,1)S(1)}, bf16[2,2,128,512]{3,2,1,0:T(8,128)(2,1)S(1)}, u32[]{:S(2)}, u32[]{:S(2)}) collective-permute-start(bf16[2,2,128,512]{3,2,1,0:T(8,128)(2,1)S(1)} %collective-permute-done.40.refs_4_), channel_id=1, source_target_pairs={{0,1},{1,0},{2,3},{3,2},{4,5},{5,4},{6,7},{7,6},{8,9},{9,8},{10,11... | collective-permute-start | bytes 1572872 | tf_op jit(solution)/shard_map/ppermute | solution.py:341
  97.8 15.5 %collective-permute-start.43 = (bf16[1,2,128,512]{3,2,1,0:T(8,128)(2,1)S(1)}, bf16[1,2,128,512]{3,2,1,0:T(8,128)(2,1)S(1)}, u32[]{:S(2)}, u32[]{:S(2)}) collective-permute-start(bf16[1,2,128,512]{3,2,1,0:T(8,128)(2,1)S(1)} %get-tuple-element.135), channel_id=1, source_target_pairs={{0,1},{1,0},{2,3},{3,2},{4,5},{5,4},{6,7},{7,6},{8,9},{9,8},{10,11... | collective-permute-start | bytes 786440 | tf_op jit(solution)/shard_map/ppermute | solution.py:343
  101.6 26.6 %collective-permute-start.35 = (bf16[2,256,512]{2,1,0:T(8,128)(2,1)S(1)}, bf16[2,256,512]{2,1,0:T(8,128)(2,1)S(1)}, u32[]{:S(2)}, u32[]{:S(2)}) collective-permute-start(bf16[2,256,512]{2,1,0:T(8,128)(2,1)S(1)} %get-tuple-element.113), channel_id=1, source_target_pairs={{0,8},{4,12},{8,0},{12,4},{16,24},{20,28},{24,16},{28,20},{1,9},{5... | collective-permute-start | bytes 1572872 | tf_op jit(solution)/shard_map/ppermute | solution.py:380
  103.0 21.0 %collective-permute-start.48 = (bf16[1,2,128,512]{3,2,1,0:T(8,128)(2,1)S(1)}, bf16[1,2,128,512]{3,2,1,0:T(8,128)(2,1)S(1)}, u32[]{:S(2)}, u32[]{:S(2)}) collective-permute-start(bf16[1,2,128,512]{3,2,1,0:T(8,128)(2,1)S(1)} %get-tuple-element.134), channel_id=1, source_target_pairs={{0,1},{1,0},{2,3},{3,2},{4,5},{5,4},{6,7},{7,6},{8,9},{9,8},{10,11... | collective-permute-start | bytes 786440 | tf_op jit(solution)/shard_map/ppermute | solution.py:344
  104.5 24.7 %collective-permute-start.36 = (bf16[2,256,512]{2,1,0:T(8,128)(2,1)S(1)}, bf16[2,256,512]{2,1,0:T(8,128)(2,1)S(1)}, u32[]{:S(2)}, u32[]{:S(2)}) collective-permute-start(bf16[2,256,512]{2,1,0:T(8,128)(2,1)S(1)} %get-tuple-element.114), channel_id=1, source_target_pairs={{0,16},{4,20},{8,24},{12,28},{16,0},{20,4},{24,8},{28,12},{1,17},{... | collective-permute-start | bytes 1572872 | tf_op jit(solution)/shard_map/ppermute | solution.py:381
  107.7 16.0 %collective-permute-start.25 = (bf16[136,512]{1,0:T(8,128)(2,1)S(1)}, bf16[136,512]{1,0:T(8,128)(2,1)S(1)}, u32[]{:S(2)}, u32[]{:S(2)}) collective-permute-start(bf16[136,512]{1,0:T(8,128)(2,1)S(1)} %get-tuple-element.102), channel_id=1, source_target_pairs={{0,20},{4,16},{8,28},{12,24},{16,4},{20,0},{24,12},{28,8},{1,21},{... | collective-permute-start | bytes 417800 | tf_op jit(solution)/shard_map/ppermute | solution.py:67
  113.3 12.9 %collective-permute-start.26 = (bf16[136,512]{1,0:T(8,128)(2,1)S(1)}, bf16[136,512]{1,0:T(8,128)(2,1)S(1)}, u32[]{:S(2)}, u32[]{:S(2)}) collective-permute-start(bf16[136,512]{1,0:T(8,128)(2,1)S(1)} %get-tuple-element.103), channel_id=1, source_target_pairs={{0,24},{4,28},{8,16},{12,20},{16,8},{20,12},{24,0},{28,4},{1,25},{... | collective-permute-start | bytes 417800 | tf_op jit(solution)/shard_map/ppermute | solution.py:67
  126.2 12.2 %collective-permute-start.49 = (bf16[2,128,512]{2,1,0:T(8,128)(2,1)S(1)}, bf16[2,128,512]{2,1,0:T(8,128)(2,1)S(1)}, u32[]{:S(2)}, u32[]{:S(2)}) collective-permute-start(bf16[2,128,512]{2,1,0:T(8,128)(2,1)S(1)} %get-tuple-element.128), channel_id=1, source_target_pairs={{0,8},{4,12},{8,0},{12,4},{16,24},{20,28},{24,16},{28,20},{1,9},{5... | collective-permute-start | bytes 786440 | tf_op jit(solution)/shard_map/ppermute | solution.py:380
  128.2 13.4 %collective-permute-start.50 = (bf16[2,128,512]{2,1,0:T(8,128)(2,1)S(1)}, bf16[2,128,512]{2,1,0:T(8,128)(2,1)S(1)}, u32[]{:S(2)}, u32[]{:S(2)}) collective-permute-start(bf16[2,128,512]{2,1,0:T(8,128)(2,1)S(1)} %get-tuple-element.129), channel_id=1, source_target_pairs={{0,16},{4,20},{8,24},{12,28},{16,0},{20,4},{24,8},{28,12},{1,17},{... | collective-permute-start | bytes 786440 | tf_op jit(solution)/shard_map/ppermute | solution.py:381
  129.2 14.3 %collective-permute-start.27 = (bf16[136,512]{1,0:T(8,128)(2,1)S(1)}, bf16[136,512]{1,0:T(8,128)(2,1)S(1)}, u32[]{:S(2)}, u32[]{:S(2)}) collective-permute-start(bf16[136,512]{1,0:T(8,128)(2,1)S(1)} %get-tuple-element.104), channel_id=1, source_target_pairs={{0,28},{4,24},{8,20},{12,16},{16,12},{20,8},{24,4},{28,0},{1,29},{... | collective-permute-start | bytes 417800 | tf_op jit(solution)/shard_map/ppermute | solution.py:67
  132.8 20.8 %collective-permute-start.37 = (bf16[256,512]{1,0:T(8,128)(2,1)S(1)}, bf16[256,512]{1,0:T(8,128)(2,1)S(1)}, u32[]{:S(2)}, u32[]{:S(2)}) collective-permute-start(bf16[256,512]{1,0:T(8,128)(2,1)S(1)} %get-tuple-element.117), channel_id=1, source_target_pairs={{0,16},{4,20},{8,24},{12,28},{16,0},{20,4},{24,8},{28,12},{1,17},{... | collective-permute-start | bytes 786440 | tf_op jit(solution)/shard_map/ppermute | solution.py:394
  133.8 19.9 %collective-permute-start.38 = (bf16[256,512]{1,0:T(8,128)(2,1)S(1)}, bf16[256,512]{1,0:T(8,128)(2,1)S(1)}, u32[]{:S(2)}, u32[]{:S(2)}) collective-permute-start(bf16[256,512]{1,0:T(8,128)(2,1)S(1)} %get-tuple-element.118), channel_id=1, source_target_pairs={{0,8},{4,12},{8,0},{12,4},{16,24},{20,28},{24,16},{28,20},{1,9},{5... | collective-permute-start | bytes 786440 | tf_op jit(solution)/shard_map/ppermute | solution.py:395
  (37 other events, 353.6 us)
